TPU v7x, 32 devices: a whole 2x2x4 slice. The times are simulated.
32 devices in a mesh: dp: 8 (over y, x, core), mp: 4 (over z).
Axes of the slice: x: 2, y: 2, z: 4, core: 2. Of those that a mesh axis runs over, the one named last changes fastest.
Arguments:
- inputs: bfloat16 [8, 1024, 1024], P('dp', 'mp')
- segments: int32 [8, 1024], P('dp'), may hold values from 0 to 5, never falling along the last dimension, each value on 1 to 512 neighbouring positions
- positions: int32 [8, 1024], P('dp'), may hold values from 0 to 1279, as said below
- boxes: int32 [2, 8, 1024], P(None, 'dp'), may hold values from 0 to 255
- pad_mask: int32 [8, 1024], P('dp'), may hold values from 0 to 1, as said below
- w_qkv: bfloat16 [3, 1024, 1024], P(None, 'dp', 'mp'), may hold values from -0.09375 to 0.09375
- w_out: bfloat16 [1024, 1024], P('mp', 'dp'), may hold values from -3 to 3
- w_gate_up: bfloat16 [2, 1024, 2816], P(None, 'dp', 'mp'), may hold values from -0.1875 to 0.1875
- w_down: bfloat16 [2816, 1024], P('mp', 'dp'), may hold values from -0.109375 to 0.109375
- bias_tables: bfloat16 [3, 32, 16], P(None, None, 'mp'), may hold values from -4 to 4
- gains: bfloat16 [2, 1024], replicated, may hold values from 0.25 to 1.75
- out_grad: bfloat16 [8, 1024, 1024], P('dp', 'mp'), may hold values from -6 to 6
Outputs:
- out: bfloat16 [8, 1024, 1024], P('dp', 'mp')
- input_grad: bfloat16 [8, 1024, 1024], P('dp', 'mp')
- w_qkv_grad: float32 [3, 1024, 1024], P(None, 'dp', 'mp')
- w_out_grad: float32 [1024, 1024], P('mp', 'dp')
- w_gate_up_grad: float32 [2, 1024, 2816], P(None, 'dp', 'mp')
- w_down_grad: float32 [2816, 1024], P('mp', 'dp')
- table_grad: float32 [3, 32, 16], P(None, 'dp', 'mp')
- gain_grad: float32 [2, 1024], P(None, ('dp', 'mp'))
Inputs may be any that keep to these rules, and one draw needn't show every extreme that they name: Along each row positions start at 0 and rise by 1 or 2 from token to token; the last token of every row is at 1279. `pad_mask`: in each row the 1s form a leading run and the 0s the rest.
All inputs are finite; a program needn't handle non-finite values.
Results may differ from a plain program's by a relative error of at most 0.018.
Values may be sent and summed in bfloat16 or wider, within the bound.
No kernel may reach another device: no remote copies, remote signals or barrier semaphores. Data moves between devices by JAX's collectives and lax.ppermute only.
A program may use at most 320 MiB of HBM per device.

v0:
```python
import jax
import jax.numpy as jnp
from jax import lax
from jax.sharding import PartitionSpec as P

NB = 32


epsilon = 1e-06
gelu_coefficient = 0.7978845608028654
thresholds = (12, 16, 23, 32, 46, 64, 91)


def bucket_of(distance):
    magnitude = jnp.abs(distance)
    stepped = 8 + sum(((magnitude >= boundary).astype(jnp.int32) for boundary in thresholds))
    return jnp.where(magnitude < 8, magnitude, stepped) + 16 * (distance > 0).astype(jnp.int32)


def rms_scale(row_values, gain_row):
    return (
        row_values
        * lax.rsqrt(jnp.mean(row_values * row_values, axis=-1, keepdims=True) + epsilon)
        * gain_row
    )


def gelu_tanh(values):
    return (
        0.5
        * values
        * (1.0 + jnp.tanh(gelu_coefficient * (values + 0.044715 * values * values * values)))
    )


def gated_unit(gate_rows, up_rows):
    return gelu_tanh(gate_rows) * up_rows


def pair_layout(row_labels, first_row, block_rows):
    segment, position, across, downward, padding = row_labels
    length = segment.shape[0]

    def block_of(values):
        return values[first_row : first_row + block_rows]

    buckets = jnp.stack(
        [
            bucket_of(position[None, :] - block_of(position)[:, None]),
            bucket_of(across[None, :] - block_of(across)[:, None]),
            bucket_of(downward[None, :] - block_of(downward)[:, None]),
        ]
    )
    query_index = first_row + lax.broadcasted_iota(jnp.int32, (block_rows, length), 0)
    key_index = lax.broadcasted_iota(jnp.int32, (block_rows, length), 1)
    allowed = (block_of(segment)[:, None] == segment[None, :]) & (
        (padding[None, :] == 1) | (query_index == key_index)
    )
    return (buckets, allowed)


def table_bias(buckets, tables):
    head_count = tables.shape[2]
    looked = jnp.zeros((head_count,) + buckets.shape[1:], jnp.float32)
    for kind_index in range(3):
        kind_buckets = buckets[kind_index][None]
        for number in range(NB):
            looked = looked + jnp.where(
                kind_buckets == number, tables[kind_index, number][:, None, None], 0.0
            )
    return looked


def table_sums(buckets, scores_grad):
    grad_values = scores_grad.astype(jnp.float32)
    kind_sums = []
    for kind_index in range(3):
        kind_buckets = buckets[kind_index][None]
        number_sums = [
            jnp.sum(jnp.where(kind_buckets == number, grad_values, 0.0), axis=(1, 2))
            for number in range(NB)
        ]
        kind_sums.append(jnp.stack(number_sums))
    return jnp.stack(kind_sums)


def masked_scores(query_block, key_heads, tables, buckets, allowed):
    head_count = key_heads.shape[1]
    block_heads = query_block.reshape(query_block.shape[0], head_count, -1)
    raw_scores = jnp.einsum(
        "qhe,khe->hqk", block_heads, key_heads, preferred_element_type=jnp.float32
    )
    scores = raw_scores + table_bias(buckets, tables)
    return (jnp.where(allowed[None], scores, -1e30), block_heads)


def attention_forward(projected, labels, tables):
    head_count = tables.shape[2]
    length = projected.shape[2]
    block_rows = min(512, length)

    def one_row(row_items):
        queries, key_rows, values = (row_items[0], row_items[1], row_items[2])
        row_labels = row_items[3:]
        key_heads = key_rows.reshape(length, head_count, -1)
        value_heads = values.reshape(length, head_count, -1)
        outputs = []
        log_sums = []
        for first_row in range(0, length, block_rows):
            buckets, allowed = pair_layout(row_labels, first_row, block_rows)
            scores, block_heads = masked_scores(
                queries[first_row : first_row + block_rows], key_heads, tables, buckets, allowed
            )
            row_max = jnp.max(scores, axis=2, keepdims=True)
            exponent = jnp.exp(scores - row_max)
            denominator = jnp.sum(exponent, axis=2, keepdims=True)
            weights_low = (exponent / denominator).astype(jnp.bfloat16)
            mixed_rows = jnp.einsum(
                "hqk,khe->qhe", weights_low, value_heads, preferred_element_type=jnp.float32
            )
            outputs.append(mixed_rows.reshape(block_rows, -1).astype(jnp.bfloat16))
            log_sums.append((row_max + jnp.log(denominator))[:, :, 0])
        return (jnp.concatenate(outputs, axis=0), jnp.concatenate(log_sums, axis=1))

    return lax.map(one_row, (projected[0], projected[1], projected[2]) + tuple(labels))


def attention_backward(projected, mixed_grad, log_sums, labels, tables):
    head_count = tables.shape[2]
    length = projected.shape[2]
    block_rows = min(512, length)

    def one_row(row_items):
        queries, key_rows, values, gradient_rows, row_lse = (
            row_items[0],
            row_items[1],
            row_items[2],
            row_items[3],
            row_items[4],
        )
        row_labels = row_items[5:]
        key_heads = key_rows.reshape(length, head_count, -1)
        value_heads = values.reshape(length, head_count, -1)
        key_grad = jnp.zeros(key_heads.shape, jnp.float32)
        value_grad = jnp.zeros(value_heads.shape, jnp.float32)
        table_grad = jnp.zeros(tables.shape, jnp.float32)
        query_grads = []
        for first_row in range(0, length, block_rows):
            buckets, allowed = pair_layout(row_labels, first_row, block_rows)
            scores, block_heads = masked_scores(
                queries[first_row : first_row + block_rows], key_heads, tables, buckets, allowed
            )
            probabilities = jnp.exp(scores - row_lse[:, first_row : first_row + block_rows, None])
            grad_heads = gradient_rows[first_row : first_row + block_rows].reshape(
                block_rows, head_count, -1
            )
            value_grad = value_grad + jnp.einsum(
                "hqk,qhe->khe",
                probabilities.astype(jnp.bfloat16),
                grad_heads,
                preferred_element_type=jnp.float32,
            )
            probs_grad = jnp.einsum(
                "qhe,khe->hqk", grad_heads, value_heads, preferred_element_type=jnp.float32
            )
            scores_grad = (
                probabilities
                * (probs_grad - jnp.sum(probs_grad * probabilities, axis=2, keepdims=True))
            ).astype(jnp.bfloat16)
            query_grad = jnp.einsum(
                "hqk,khe->qhe", scores_grad, key_heads, preferred_element_type=jnp.float32
            )
            query_grads.append(query_grad.reshape(block_rows, -1).astype(jnp.bfloat16))
            key_grad = key_grad + jnp.einsum(
                "hqk,qhe->khe", scores_grad, block_heads, preferred_element_type=jnp.float32
            )
            table_grad = table_grad + table_sums(buckets, scores_grad)
        stacked = jnp.stack(
            [
                jnp.concatenate(query_grads, axis=0),
                key_grad.reshape(length, -1).astype(jnp.bfloat16),
                value_grad.reshape(length, -1).astype(jnp.bfloat16),
            ]
        )
        return (stacked, table_grad)

    stacked, table_grads = lax.map(
        one_row, (projected[0], projected[1], projected[2], mixed_grad, log_sums) + tuple(labels)
    )
    return (stacked, jnp.sum(table_grads, axis=0))


def on_device(
    inputs,
    segments,
    positions,
    boxes,
    pad_mask,
    w_qkv,
    w_out,
    w_gate_up,
    w_down,
    bias_tables,
    gains,
    out_grad,
):
    labels = (segments, positions, boxes[0], boxes[1], pad_mask)
    gain_values = gains.astype(jnp.float32)
    table_values = bias_tables.astype(jnp.float32)

    def attn_weights():
        return (
            lax.all_gather(w_qkv, "dp", axis=1, tiled=True),
            lax.all_gather(w_out, "dp", axis=1, tiled=True),
        )

    def ffn_weights():
        return (
            lax.all_gather(w_gate_up, "dp", axis=1, tiled=True),
            lax.all_gather(w_down, "dp", axis=1, tiled=True),
        )

    def attn_rows(normed):
        return lax.all_gather(normed, "mp", axis=1, tiled=True)

    def ffn_rows(normed):
        return lax.all_gather(normed, "mp", axis=1, tiled=True)

    input_rows = inputs.astype(jnp.float32)
    query_key_value_full, output_weight_full = attn_weights()
    complete_first_gain = attn_rows(rms_scale(input_rows, gain_values[0]).astype(jnp.bfloat16))
    projected = jnp.einsum(
        "bwh,thk->tbwk",
        complete_first_gain,
        query_key_value_full,
        preferred_element_type=jnp.float32,
    ).astype(jnp.bfloat16)
    mixed_output, log_sums = attention_forward(projected, labels, table_values)
    attention_residual = jnp.einsum(
        "obu,uh->obh", mixed_output, output_weight_full, preferred_element_type=jnp.float32
    )
    middle = input_rows + lax.psum_scatter(
        attention_residual, "mp", scatter_dimension=1, tiled=True
    )
    gate_up_weight_full, down_weight_full = ffn_weights()
    complete_second_gain = ffn_rows(rms_scale(middle, gain_values[1]).astype(jnp.bfloat16))
    gate_up = jnp.einsum(
        "eki,yig->yekg",
        complete_second_gain,
        gate_up_weight_full,
        preferred_element_type=jnp.float32,
    )
    hidden_state = gated_unit(gate_up[0], gate_up[1]).astype(jnp.bfloat16)
    feedforward_residual = jnp.einsum(
        "iva,ap->ivp", hidden_state, down_weight_full, preferred_element_type=jnp.float32
    )
    result = (
        middle
        + lax.psum_scatter(
            feedforward_residual.astype(jnp.bfloat16), "mp", scatter_dimension=1, tiled=True
        ).astype(jnp.float32)
    ).astype(jnp.bfloat16)
    gradient_rows = lax.all_gather(out_grad, "mp", axis=1, tiled=True)
    gate_up_weight_used, down_weight_used = ffn_weights()
    complete_second_gain_used = ffn_rows(rms_scale(middle, gain_values[1]).astype(jnp.bfloat16))
    gate_up_vals = jnp.einsum(
        "eki,yig->yekg",
        complete_second_gain_used,
        gate_up_weight_used,
        preferred_element_type=jnp.float32,
    )
    hidden_state_used = gated_unit(gate_up_vals[0], gate_up_vals[1]).astype(jnp.bfloat16)
    hidden_state_gradient = jnp.einsum(
        "ybz,oz->ybo", gradient_rows, down_weight_used, preferred_element_type=jnp.float32
    )
    unused_value, gated_back = jax.vjp(gated_unit, gate_up_vals[0], gate_up_vals[1])
    gate_grad, up_grad = gated_back(hidden_state_gradient)
    gate_up_gradient = jnp.stack([gate_grad, up_grad]).astype(jnp.bfloat16)
    down_weight_grad = jnp.einsum(
        "zci,zcj->ij", hidden_state_used, gradient_rows, preferred_element_type=jnp.float32
    )
    gate_up_weight_grad = jnp.einsum(
        "bhu,qbhz->quz",
        complete_second_gain_used,
        gate_up_gradient,
        preferred_element_type=jnp.float32,
    )
    two_term = jnp.einsum(
        "gwzh,gih->wzi", gate_up_gradient, gate_up_weight_used, preferred_element_type=jnp.float32
    )
    normed_two_grad = lax.psum_scatter(two_term, "mp", scatter_dimension=1, tiled=True)
    ffn_grads = (
        lax.psum_scatter(
            gate_up_weight_grad.astype(jnp.bfloat16), "dp", scatter_dimension=1, tiled=True
        ).astype(jnp.float32),
        lax.psum_scatter(
            down_weight_grad.astype(jnp.bfloat16), "dp", scatter_dimension=1, tiled=True
        ).astype(jnp.float32),
    )
    unused_two, norm_back_two = jax.vjp(rms_scale, middle, gain_values[1])
    middle_part, gain_two_grad = norm_back_two(normed_two_grad)
    middle_grad = middle_part + out_grad.astype(jnp.float32)
    attention_gradient_rows = lax.all_gather(
        middle_grad.astype(jnp.bfloat16), "mp", axis=1, tiled=True
    )
    query_key_value_used, output_weight_used = attn_weights()
    complete_first_gain_used = attn_rows(rms_scale(input_rows, gain_values[0]).astype(jnp.bfloat16))
    projected_use = jnp.einsum(
        "bwh,thk->tbwk",
        complete_first_gain_used,
        query_key_value_used,
        preferred_element_type=jnp.float32,
    ).astype(jnp.bfloat16)
    mixed_grad = jnp.einsum(
        "owh,bh->owb",
        attention_gradient_rows,
        output_weight_used,
        preferred_element_type=jnp.float32,
    ).astype(jnp.bfloat16)
    out_weight_grad = jnp.einsum(
        "kaz,kaw->zw", mixed_output, attention_gradient_rows, preferred_element_type=jnp.float32
    )
    projection_gradient, table_grad = attention_backward(
        projected_use, mixed_grad, log_sums, labels, table_values
    )
    qkv_weight_grad = jnp.einsum(
        "fxy,fixg->iyg",
        complete_first_gain_used,
        projection_gradient,
        preferred_element_type=jnp.float32,
    )
    one_term = jnp.einsum(
        "ypwk,pzk->ywz",
        projection_gradient,
        query_key_value_used,
        preferred_element_type=jnp.float32,
    )
    normed_one_grad = lax.psum_scatter(
        one_term.astype(jnp.bfloat16), "mp", scatter_dimension=1, tiled=True
    ).astype(jnp.float32)
    attn_grads = (
        lax.psum_scatter(
            qkv_weight_grad.astype(jnp.bfloat16), "dp", scatter_dimension=1, tiled=True
        ).astype(jnp.float32),
        lax.psum_scatter(
            out_weight_grad.astype(jnp.bfloat16), "dp", scatter_dimension=1, tiled=True
        ).astype(jnp.float32),
        lax.psum_scatter(
            table_grad.astype(jnp.bfloat16), "dp", scatter_dimension=1, tiled=True
        ).astype(jnp.float32),
    )
    unused_one, norm_back_one = jax.vjp(rms_scale, input_rows, gain_values[0])
    input_part, gain_one_grad = norm_back_one(normed_one_grad)
    input_grad = (input_part + middle_grad).astype(jnp.bfloat16)
    gain_grad = lax.psum_scatter(
        jnp.stack([gain_one_grad, gain_two_grad]), ("dp", "mp"), scatter_dimension=1, tiled=True
    )
    return (
        result,
        input_grad,
        attn_grads[0],
        attn_grads[1],
        ffn_grads[0],
        ffn_grads[1],
        attn_grads[2],
        gain_grad,
    )


def solution(mesh):
    placed = (
        P("dp", "mp", None),
        P("dp", None),
        P("dp", None),
        P(None, "dp", None),
        P("dp", None),
        P(None, "dp", "mp"),
        P("mp", "dp"),
        P(None, "dp", "mp"),
        P("mp", "dp"),
        P(None, None, "mp"),
        P(),
        P("dp", "mp", None),
    )
    return jax.shard_map(
        on_device,
        mesh=mesh,
        in_specs=placed,
        out_specs=(
            P("dp", "mp", None),
            P("dp", "mp", None),
            P(None, "dp", "mp"),
            P("mp", "dp"),
            P(None, "dp", "mp"),
            P("mp", "dp"),
            P(None, "dp", "mp"),
            P(None, ("dp", "mp")),
        ),
        check_vma=False,
    )
```

profile of v0, /device:TPU:0, one launch (start us, length us, event | category | flops | bytes accessed | tf_op | source)
XLA Modules:
  0.0 1428.5 jit_solution(11029591934329853670)
XLA Ops:
  7.2 1.7 copy.35
  12.8 2.0 fusion.329
  17.0 30.3 %broadcast_compare_fusion.164 = (pred[512,1024]{1,0:T(8,128)(4,1)}, pred[512,1024]{1,0:T(8,128)(4,1)}, pred[512,1024]{1,0:T(8,128)(4,1)}, pred[512,1024]{1,0:T(8...) fusion(s32[512]{0:T(512)S(1)} %bitcast.458, ...), kind=kLoop, calls=%fused_computation.736 | loop fusion | flops 62914560 | bytes 33562624 | tf_op jit(solution)/shard_map/while/body/eval_jaxpr/eq | solution.py:69
  47.3 30.6 %broadcast_compare_fusion.165 = (pred[512,1024]{1,0:T(8,128)(4,1)}, pred[512,1024]{1,0:T(8,128)(4,1)}, pred[512,1024]{1,0:T(8,128)(4,1)}, pred[512,1024]{1,0:T(8...) fusion(s32[512]{0:T(512)S(1)} %bitcast.456, ...), kind=kLoop, calls=%fused_computation.737 | loop fusion | flops 62914560 | bytes 33562624 | tf_op jit(solution)/shard_map/while/body/eval_jaxpr/eq | solution.py:69
  78.0 30.4 %broadcast_compare_fusion.166 = (pred[512,1024]{1,0:T(8,128)(4,1)}, pred[512,1024]{1,0:T(8,128)(4,1)S(1)}, pred[512,1024]{1,0:T(8,128)(4,1)S(1)}, pred[512,1024]...) fusion(s32[512]{0:T(512)S(1)} %bitcast.452, ...), kind=kLoop, calls=%fused_computation.738 | loop fusion | flops 62914560 | bytes 33562624 | tf_op jit(solution)/shard_map/while/body/eval_jaxpr/eq | solution.py:69
  114.2 12.7 all_gather.32
  126.9 2.1 fusion.282
  129.3 4.0 fusion.298
  135.2 127.4 %fusion.364 = (f32[4,512]{1,0:T(4,128)S(1)}, f32[4,512,1024]{2,1,0:T(8,128)S(1)}) fusion(f32[4]{0:T(128)} %get-tuple-element.299, pred[512,1024]{1,0:T(8,128)(4,1)} %get-tuple-element.508, f32[4]{0:T(128)} %get-tuple-element.300, pred[512,1024]{1,0:T(8,128)(4,1)} %get-tuple-element.507, f32[4]{0:T(128)} %get-tuple-element.301, ...), kind=kOutput, calls=%fused_computation.900 | convolution fusion | flops 675280896 | bytes 60040704 | tf_op jit(solution)/shard_map/while/body/eval_jaxpr/qhe,khe->hqk/dot_general | solution.py:90
  262.6 1.7 fusion.192
  264.6 2.6 fusion.328
  267.8 115.9 %fusion.363 = (f32[4,512]{1,0:T(4,128)S(1)}, f32[4,512,1024]{2,1,0:T(8,128)S(1)}) fusion(f32[4]{0:T(128)} %get-tuple-element.299, pred[512,1024]{1,0:T(8,128)(4,1)} %get-tuple-element.677, f32[4]{0:T(128)} %get-tuple-element.300, pred[512,1024]{1,0:T(8,128)(4,1)} %get-tuple-element.678, f32[4]{0:T(128)} %get-tuple-element.301, ...), kind=kOutput, calls=%fused_computation.899 | convolution fusion | flops 675280896 | bytes 60040704 | tf_op jit(solution)/shard_map/while/body/eval_jaxpr/qhe,khe->hqk/dot_general | solution.py:90
  383.8 1.7 fusion.193
  385.5 1.9 fusion.327
  388.2 2.7 convolution_bitcast_fusion.2
  391.5 76.6 %reduce-scatter.21.cloned.1.call-done = f32[1,256,1024]{2,1,0:T(8,128)} async-done(((f32[1,1024,1024]{2,1,0:T(8,128)}), f32[1,256,1024]{2,1,0:T(8,128)}) %reduce-scatter.21.cloned.1.call-update) | async-done | bytes 1048592 | tf_op jit(solution)/shard_map/reduce_scatter | solution.py:242
  471.9 30.3 %all-gather.14.cloned.1.call-done = bf16[2,1024,704]{1,2,0:T(8,128)(2,1)} async-done(((bf16[2,128,704]{1,2,0:T(8,128)(2,1)}), bf16[2,1024,704]{1,2,0:T(8,128)(2,1)}) %all-gather.14.cloned.1.call-update) | async-done | bytes 2883600 | tf_op jit(solution)/shard_map/all_gather | solution.py:219
  502.2 48.0 %all-gather.12.cloned.1.call-done = bf16[1,1024,1024]{2,1,0:T(8,128)(2,1)} async-done(((bf16[1,256,1024]{2,1,0:T(8,128)(2,1)}), bf16[1,1024,1024]{2,1,0:T(8,128)(2,1)}) %all-gather.12.cloned.1.call-update) | async-done | bytes 2097168 | tf_op jit(solution)/shard_map/all_gather | solution.py:227
  550.2 8.1 convolution_bitcast_fusion
  558.4 17.8 %all-gather.16.cloned.1.call-done = bf16[704,1024]{1,0:T(8,128)(2,1)} async-done(((bf16[704,128]{1,0:T(8,128)(2,1)}), bf16[704,1024]{1,0:T(8,128)(2,1)}) %all-gather.16.cloned.1.call-update) | async-done | bytes 1441808 | tf_op jit(solution)/shard_map/all_gather | solution.py:220
  576.2 47.6 %all-gather.18.cloned.1.call-done = bf16[1,1024,1024]{2,1,0:T(8,128)(2,1)} async-done(((bf16[1,256,1024]{2,1,0:T(8,128)(2,1)}), bf16[1,1024,1024]{2,1,0:T(8,128)(2,1)}) %all-gather.18.cloned.1.call-update) | async-done | bytes 2097168 | tf_op jit(solution)/shard_map/all_gather | solution.py:263
  623.8 7.9 fusion.308
  633.3 5.0 convolution_bitcast_fusion.1
  638.3 75.6 %reduce-scatter.25.cloned.1.call-done = f32[1,256,1024]{2,1,0:T(8,128)} async-done(((f32[1,1024,1024]{2,1,0:T(8,128)}), f32[1,256,1024]{2,1,0:T(8,128)}) %reduce-scatter.25.cloned.1.call-update) | async-done | bytes 1048592 | tf_op jit(solution)/shard_map/reduce_scatter | solution.py:291
  715.4 2.3 fusion.354
  718.0 6.4 fusion.291
  724.4 2.6 copy.244
  727.2 7.2 convert_bitcast_fusion
  734.4 8.7 copy.242
  743.1 7.6 reshape.6784
  750.8 13.6 all-gather.20.cloned.1.call-done
  764.4 2.4 fusion.324
  766.8 5.9 fusion.196
  772.7 6.9 multiply_reduce_fusion
  779.6 1.5 fusion.319
  781.1 2.1 copy.240
  783.2 6.5 multiply_reduce_fusion.1
  789.7 4.9 fusion.312
  795.6 33.3 %fusion.31 = (f32[4]{0:T(128)}, f32[4]{0:T(128)}, f32[4]{0:T(128)}, f32[4]{0:T(128)}, f32[4]{0:T(128)}, /*index=5*/f32[4]{0:T(128)}, f32[4]{0:T(128)}, f32[4]{0:...) fusion(pred[512,1024]{1,0:T(8,128)(4,1)} %get-tuple-element.444, ...), kind=kLoop, calls=%fused_computation.223 | loop fusion | flops 85983168 | bytes 30425376 | tf_op jit(solution)/shard_map/while/body/eval_jaxpr/reduce_sum | solution.py:80
  829.0 2.0 copy-done.2
  833.2 34.0 %fusion.127 = (f32[4]{0:T(128)}, f32[4]{0:T(128)}, f32[4]{0:T(128)}, f32[4]{0:T(128)}, f32[4]{0:T(128)}, /*index=5*/f32[4]{0:T(128)}, f32[4]{0:T(128)}, f32[4]{0...) fusion(pred[512,1024]{1,0:T(8,128)(4,1)S(1)} %copy-done.13, ...), kind=kLoop, calls=%fused_computation.319 | loop fusion | flops 85983168 | bytes 30425376 | tf_op jit(solution)/shard_map/while/body/eval_jaxpr/reduce_sum | solution.py:80
  867.2 1.9 copy-done
  871.4 3.1 fusion.367
  874.6 3.8 fusion.315
  881.5 4.9 fusion.295
  886.4 4.2 copy.238
  890.6 3.2 copy.250
  893.8 4.7 fusion.294
  899.8 6.7 convert_bitcast_fusion.1
  911.2 2.0 convert_element_type.4671
  913.2 23.0 %fusion.30 = (f32[4]{0:T(128)S(1)}, f32[4]{0:T(128)S(1)}, f32[4]{0:T(128)S(1)}, f32[4]{0:T(128)S(1)}, f32[4]{0:T(128)S(1)}, /*index=5*/f32[4]{0:T(128)S(1)}, f32...) fusion(bf16[4,512,1024]{2,1,0:T(8,128)(2,1)} %copy-done.2, ...), kind=kLoop, calls=%fused_computation.222 | loop fusion | flops 77594560 | bytes 13631776 | tf_op jit(solution)/shard_map/while/body/eval_jaxpr/reduce_sum | solution.py:80
  936.5 23.2 %fusion.63 = (f32[4]{0:T(128)S(1)}, f32[4]{0:T(128)S(1)}, f32[4]{0:T(128)S(1)}, f32[4]{0:T(128)S(1)}, f32[4]{0:T(128)S(1)}, /*index=5*/f32[4]{0:T(128)S(1)}, f32...) fusion(bf16[4,512,1024]{2,1,0:T(8,128)(2,1)S(1)} %copy-done.3, ...), kind=kLoop, calls=%fused_computation.255 | loop fusion | flops 77594560 | bytes 13631776 | tf_op jit(solution)/shard_map/while/body/eval_jaxpr/reduce_sum | solution.py:80
  959.9 21.6 %fusion.95 = (f32[4]{0:T(128)S(1)}, f32[4]{0:T(128)S(1)}, f32[4]{0:T(128)S(1)}, f32[4]{0:T(128)S(1)}, f32[4]{0:T(128)S(1)}, /*index=5*/f32[4]{0:T(128)S(1)}, f32...) fusion(bf16[4,512,1024]{2,1,0:T(8,128)(2,1)S(1)} %copy-done.3, ...), kind=kLoop, calls=%fused_computation.287 | loop fusion | flops 77594560 | bytes 13631776 | tf_op jit(solution)/shard_map/while/body/eval_jaxpr/reduce_sum | solution.py:80
  981.7 23.6 %fusion = (f32[4]{0:T(128)S(1)}, f32[4]{0:T(128)S(1)}, f32[4]{0:T(128)}, f32[4]{0:T(128)}, f32[4]{0:T(128)}, /*index=5*/f32[4]{0:T(128)S(1)}, f32[4]{0:T(128)S(1...) fusion(bf16[4,512,1024]{2,1,0:T(8,128)(2,1)S(1)} %copy-done.3, ...), kind=kLoop, calls=%fused_computation.192 | loop fusion | flops 77594560 | bytes 13631776 | tf_op jit(solution)/shard_map/while/body/eval_jaxpr/reduce_sum | solution.py:80
  1005.5 15.9 %fusion.94 = (f32[4]{0:T(128)}, f32[4]{0:T(128)}, f32[4]{0:T(128)}, f32[4]{0:T(128)}, f32[4]{0:T(128)}, /*index=5*/f32[4]{0:T(128)}, f32[4]{0:T(128)}, f32[4]{0:...) fusion(bf16[4,512,1024]{2,1,0:T(8,128)(2,1)S(1)} %copy-done.3, pred[512,1024]{1,0:T(8,128)(4,1)S(1)} %copy-done.57, ...), kind=kLoop, calls=%fused_computation.286 | loop fusion | flops 54525904 | bytes 14680256 | tf_op jit(solution)/shard_map/while/body/eval_jaxpr/reduce_sum | solution.py:80
  1021.6 23.4 %fusion.126 = (f32[4]{0:T(128)}, f32[4]{0:T(128)}, f32[4]{0:T(128)}, f32[4]{0:T(128)}, f32[4]{0:T(128)}, /*index=5*/f32[4]{0:T(128)}, f32[4]{0:T(128)}, f32[4]{0...) fusion(bf16[4,512,1024]{2,1,0:T(8,128)(2,1)S(1)} %copy-done.1, ...), kind=kLoop, calls=%fused_computation.318 | loop fusion | flops 77594560 | bytes 13631776 | tf_op jit(solution)/shard_map/while/body/eval_jaxpr/reduce_sum | solution.py:80
  1045.3 23.5 %fusion.159 = (f32[4]{0:T(128)}, f32[4]{0:T(128)}, f32[4]{0:T(128)}, f32[4]{0:T(128)}, f32[4]{0:T(128)}, /*index=5*/f32[4]{0:T(128)}, f32[4]{0:T(128)}, f32[4]{0...) fusion(bf16[4,512,1024]{2,1,0:T(8,128)(2,1)S(1)} %copy-done.1, ...), kind=kLoop, calls=%fused_computation.351 | loop fusion | flops 77594560 | bytes 13631776 | tf_op jit(solution)/shard_map/while/body/eval_jaxpr/reduce_sum | solution.py:80
  1069.0 22.5 %fusion.191 = (f32[4]{0:T(128)}, f32[4]{0:T(128)}, f32[4]{0:T(128)}, f32[4]{0:T(128)}, f32[4]{0:T(128)}, /*index=5*/f32[4]{0:T(128)}, f32[4]{0:T(128)}, f32[4]{0...) fusion(bf16[4,512,1024]{2,1,0:T(8,128)(2,1)S(1)} %copy-done.1, ...), kind=kLoop, calls=%fused_computation.383 | loop fusion | flops 77594560 | bytes 13631776 | tf_op jit(solution)/shard_map/while/body/eval_jaxpr/reduce_sum | solution.py:80
  1118.6 23.8 %fusion.96 = (f32[4]{0:T(128)}, f32[4]{0:T(128)}, f32[4]{0:T(128)}, f32[4]{0:T(128)}, f32[4]{0:T(128)}, /*index=5*/f32[4]{0:T(128)}, f32[4]{0:T(128)}, f32[4]{0:...) fusion(bf16[4,512,1024]{2,1,0:T(8,128)(2,1)} %copy-done, ...), kind=kLoop, calls=%fused_computation.288 | loop fusion | flops 77594560 | bytes 13631776 | tf_op jit(solution)/shard_map/while/body/eval_jaxpr/reduce_sum | solution.py:80
  1266.6 13.6 all-reduce
  1284.5 1.8 copy.234
  1286.3 1.5 fusion.330
  1288.9 2.7 fusion.333
  1291.7 128.5 %reduce-scatter.37.cloned.1.call-done = f32[32,2]{1,0:T(8,128)} async-done(((f32[1024,2]{1,0:T(8,128)}), f32[32,2]{1,0:T(8,128)}) %reduce-scatter.37.cloned.1.call-update) | async-done | bytes 272
  (659 shorter events, 194.9 us)
Async XLA Ops:
  7.2 121.9 %all-gather.10.cloned.1.call-start = ((), (), s32[]{:S(2)}) async-start(), calls=%async_computation.10 | async-start | bytes 1769472 | tf_op jit(solution)/shard_map/all_gather | solution.py:213
  9.0 120.1 %all-gather.8.cloned.1.call-start = ((), (), s32[]{:S(2)}) async-start(), calls=%async_computation.9 | async-start | bytes 2621440 | tf_op jit(solution)/shard_map/all_gather | solution.py:224
  14.8 453.3 %reduce-scatter.21.cloned.1.call-start = ((), (), s32[]{:S(2)}) async-start(), calls=%async_computation.11 | async-start | bytes 5242880 | tf_op jit(solution)/shard_map/reduce_scatter | solution.py:242
  47.3 30.6 %copy-start.121 = (s32[1,1024]{1,0:T(1,128)S(1)}, s32[1,1024]{1,0:T(1,128)}, u32[]{:S(2)}) copy-start(s32[1,1024]{1,0:T(1,128)} %param.14) | copy-start | bytes 12292
  77.9 30.5 %copy-start.128 = (bf16[3,32,4]{1,2,0:T(4,128)(2,1)S(1)}, bf16[3,32,4]{1,2,0:T(4,128)(2,1)}, u32[]{:S(2)}) copy-start(bf16[3,32,4]{1,2,0:T(4,128)(2,1)} %param.21) | copy-start | bytes 2308
  77.9 31.5 %copy-start.127 = (s32[1,1024]{1,0:T(1,128)S(1)}, s32[1,1024]{1,0:T(1,128)}, u32[]{:S(2)}) copy-start(s32[1,1024]{1,0:T(1,128)} %param.16) | copy-start | bytes 12292
  77.9 36.3 %copy-start.114 = (bf16[256,128]{1,0:T(8,128)(2,1)S(1)}, bf16[256,128]{1,0:T(8,128)(2,1)}, u32[]{:S(2)}) copy-start(bf16[256,128]{1,0:T(8,128)(2,1)} %param.18) | copy-start | bytes 196612
  78.0 49.0 %copy-start.122 = (s32[1,1024]{1,0:T(1,128)S(1)}, s32[1,1024]{1,0:T(1,128)}, u32[]{:S(2)}) copy-start(s32[1,1024]{1,0:T(1,128)} %param.13) | copy-start | bytes 12292
  108.4 154.1 %copy-start.19 = (pred[512,1024]{1,0:T(8,128)(4,1)}, pred[512,1024]{1,0:T(8,128)(4,1)S(1)}, u32[]{:S(2)}) copy-start(pred[512,1024]{1,0:T(8,128)(4,1)S(1)} %get-tuple-element.414) | copy-start | bytes 1572868
  108.4 154.1 %copy-start.20 = (pred[512,1024]{1,0:T(8,128)(4,1)}, pred[512,1024]{1,0:T(8,128)(4,1)S(1)}, u32[]{:S(2)}) copy-start(pred[512,1024]{1,0:T(8,128)(4,1)S(1)} %get-tuple-element.415) | copy-start | bytes 1572868
  108.4 154.1 %copy-start.21 = (pred[512,1024]{1,0:T(8,128)(4,1)}, pred[512,1024]{1,0:T(8,128)(4,1)S(1)}, u32[]{:S(2)}) copy-start(pred[512,1024]{1,0:T(8,128)(4,1)S(1)} %get-tuple-element.416) | copy-start | bytes 1572868
  108.4 154.1 %copy-start.22 = (pred[512,1024]{1,0:T(8,128)(4,1)}, pred[512,1024]{1,0:T(8,128)(4,1)S(1)}, u32[]{:S(2)}) copy-start(pred[512,1024]{1,0:T(8,128)(4,1)S(1)} %get-tuple-element.417) | copy-start | bytes 1572868
  108.4 154.1 %copy-start.23 = (pred[512,1024]{1,0:T(8,128)(4,1)}, pred[512,1024]{1,0:T(8,128)(4,1)S(1)}, u32[]{:S(2)}) copy-start(pred[512,1024]{1,0:T(8,128)(4,1)S(1)} %get-tuple-element.418) | copy-start | bytes 1572868
  111.0 151.6 %copy-start.142 = (f32[4]{0:T(128)}, f32[4]{0:T(128)S(1)}, u32[]{:S(2)}) copy-start(f32[4]{0:T(128)S(1)} %get-tuple-element.368) | copy-start | bytes 52
  111.0 151.6 %copy-start.144 = (f32[4]{0:T(128)}, f32[4]{0:T(128)S(1)}, u32[]{:S(2)}) copy-start(f32[4]{0:T(128)S(1)} %get-tuple-element.369) | copy-start | bytes 52
  134.1 128.5 %copy-start.106 = (bf16[1,1,512,256]{2,3,0,1:T(8,128)(2,1)}, bf16[1,1,512,256]{2,3,0,1:T(8,128)(2,1)S(1)}, u32[]{:S(2)}) copy-start(bf16[1,1,512,256]{2,3,0,1:T(8,128)(2,1)S(1)} %get-tuple-element.399) | copy-start | bytes 786436
  387.5 80.6 %copy-start.6 = (bf16[1,256,1024]{2,1,0:T(8,128)(2,1)S(1)}, bf16[1,256,1024]{2,1,0:T(8,128)(2,1)}, u32[]{:S(2)}) copy-start(bf16[1,256,1024]{2,1,0:T(8,128)(2,1)} %param.12) | copy-start | bytes 1572868
  387.5 82.1 %copy-start.113 = (f32[1,1024]{1,0:T(1,128)S(1)}, f32[1,1024]{1,0:T(1,128)}, u32[]{:S(2)}) copy-start(f32[1,1024]{1,0:T(1,128)} %get-tuple-element.607) | copy-start | bytes 12292
  390.9 111.3 %all-gather.14.cloned.1.call-start = ((), (), s32[]{:S(2)}) async-start(), calls=%async_computation.13 | async-start | bytes 3244032 | tf_op jit(solution)/shard_map/all_gather | solution.py:219
  391.4 158.8 %all-gather.12.cloned.1.call-start = ((), (), s32[]{:S(2)}) async-start(), calls=%async_computation.12 | async-start | bytes 2621440 | tf_op jit(solution)/shard_map/all_gather | solution.py:227
  470.6 105.6 %all-gather.16.cloned.1.call-start = ((), (), s32[]{:S(2)}) async-start(), calls=%async_computation.14 | async-start | bytes 1622016 | tf_op jit(solution)/shard_map/all_gather | solution.py:220
  471.1 152.7 %all-gather.18.cloned.1.call-start = ((), (), s32[]{:S(2)}) async-start(), calls=%async_computation.16 | async-start | bytes 2621440 | tf_op jit(solution)/shard_map/all_gather | solution.py:263
  471.9 242.0 %reduce-scatter.25.cloned.1.call-start = ((), (), s32[]{:S(2)}) async-start(), calls=%async_computation.17 | async-start | bytes 5242880 | tf_op jit(solution)/shard_map/reduce_scatter | solution.py:291
  633.3 82.1 %copy-start.10 = (bf16[1,256,1024]{2,1,0:T(8,128)(2,1)S(1)}, bf16[1,256,1024]{2,1,0:T(8,128)(2,1)}, u32[]{:S(2)}) copy-start(bf16[1,256,1024]{2,1,0:T(8,128)(2,1)} %param.23) | copy-start | bytes 1572868
  638.3 126.1 %all-gather.20.cloned.1.call-start = ((), (), s32[]{:S(2)}) async-start(), calls=%async_computation.18 | async-start | bytes 2621440 | tf_op jit(solution)/shard_map/all_gather | solution.py:303
  717.8 188.9 %reduce-scatter.35.cloned.1.call-start = ((), (), s32[]{:S(2)}) async-start(), calls=%async_computation.23 | async-start | bytes 1769472
  727.1 181.4 %reduce-scatter.33.cloned.1.call-start = ((), (), s32[]{:S(2)}) async-start(), calls=%async_computation.22 | async-start | bytes 3244032
  750.7 530.2 %reduce-scatter.31.cloned.1.call-start = ((), (), s32[]{:S(2)}) async-start(), calls=%async_computation.21 | async-start | bytes 589824
  795.6 37.5 %copy-start.13 = (pred[512,1024]{1,0:T(8,128)(4,1)S(1)}, pred[512,1024]{1,0:T(8,128)(4,1)}, u32[]{:S(2)}) copy-start(pred[512,1024]{1,0:T(8,128)(4,1)} %get-tuple-element.611) | copy-start | bytes 1572868
  874.5 408.1 %reduce-scatter.29.cloned.1.call-start = ((), (), s32[]{:S(2)}) async-start(), calls=%async_computation.20 | async-start | bytes 1769472
  893.8 392.5 %reduce-scatter.27.cloned.1.call-start = ((), (), s32[]{:S(2)}) async-start(), calls=%async_computation.19 | async-start | bytes 2621440 | tf_op jit(solution)/shard_map/reduce_scatter | solution.py:338
  898.5 390.4 %reduce-scatter.23.cloned.1.call-start = ((), (), s32[]{:S(2)}) async-start(), calls=%async_computation.15 | async-start | bytes 2621440 | tf_op jit(solution)/shard_map/reduce_scatter | solution.py:259
  906.6 513.6 %reduce-scatter.37.cloned.1.call-start = ((), (), s32[]{:S(2)}) async-start(), calls=%async_computation.24 | async-start | bytes 540672
  911.2 25.1 %copy-start.3 = (bf16[4,512,1024]{2,1,0:T(8,128)(2,1)S(1)}, bf16[4,512,1024]{2,1,0:T(8,128)(2,1)}, u32[]{:S(2)}) copy-start(bf16[4,512,1024]{2,1,0:T(8,128)(2,1)} %copy-done.2) | copy-start | bytes 12582916
  981.6 23.7 %copy-start.1 = (bf16[4,512,1024]{2,1,0:T(8,128)(2,1)S(1)}, bf16[4,512,1024]{2,1,0:T(8,128)(2,1)}, u32[]{:S(2)}) copy-start(bf16[4,512,1024]{2,1,0:T(8,128)(2,1)} %copy-done) | copy-start | bytes 12582916
  981.6 23.7 %copy-start.52 = (pred[512,1024]{1,0:T(8,128)(4,1)S(1)}, pred[512,1024]{1,0:T(8,128)(4,1)}, u32[]{:S(2)}) copy-start(pred[512,1024]{1,0:T(8,128)(4,1)} %get-tuple-element.502) | copy-start | bytes 1572868
  981.6 23.7 %copy-start.53 = (pred[512,1024]{1,0:T(8,128)(4,1)S(1)}, pred[512,1024]{1,0:T(8,128)(4,1)}, u32[]{:S(2)}) copy-start(pred[512,1024]{1,0:T(8,128)(4,1)} %get-tuple-element.503) | copy-start | bytes 1572868
  981.6 23.7 %copy-start.54 = (pred[512,1024]{1,0:T(8,128)(4,1)S(1)}, pred[512,1024]{1,0:T(8,128)(4,1)}, u32[]{:S(2)}) copy-start(pred[512,1024]{1,0:T(8,128)(4,1)} %get-tuple-element.504) | copy-start | bytes 1572868
  981.6 23.7 %copy-start.55 = (pred[512,1024]{1,0:T(8,128)(4,1)S(1)}, pred[512,1024]{1,0:T(8,128)(4,1)}, u32[]{:S(2)}) copy-start(pred[512,1024]{1,0:T(8,128)(4,1)} %get-tuple-element.505) | copy-start | bytes 1572868
  981.6 23.7 %copy-start.56 = (pred[512,1024]{1,0:T(8,128)(4,1)S(1)}, pred[512,1024]{1,0:T(8,128)(4,1)}, u32[]{:S(2)}) copy-start(pred[512,1024]{1,0:T(8,128)(4,1)} %get-tuple-element.506) | copy-start | bytes 1572868
  981.7 23.7 %copy-start.57 = (pred[512,1024]{1,0:T(8,128)(4,1)S(1)}, pred[512,1024]{1,0:T(8,128)(4,1)}, u32[]{:S(2)}) copy-start(pred[512,1024]{1,0:T(8,128)(4,1)} %get-tuple-element.507) | copy-start | bytes 1572868
  981.7 23.7 %copy-start.58 = (pred[512,1024]{1,0:T(8,128)(4,1)S(1)}, pred[512,1024]{1,0:T(8,128)(4,1)}, u32[]{:S(2)}) copy-start(pred[512,1024]{1,0:T(8,128)(4,1)} %get-tuple-element.678) | copy-start | bytes 1572868
  981.7 23.7 %copy-start.59 = (pred[512,1024]{1,0:T(8,128)(4,1)S(1)}, pred[512,1024]{1,0:T(8,128)(4,1)}, u32[]{:S(2)}) copy-start(pred[512,1024]{1,0:T(8,128)(4,1)} %get-tuple-element.679) | copy-start | bytes 1572868
  981.7 23.7 %copy-start.60 = (pred[512,1024]{1,0:T(8,128)(4,1)S(1)}, pred[512,1024]{1,0:T(8,128)(4,1)}, u32[]{:S(2)}) copy-start(pred[512,1024]{1,0:T(8,128)(4,1)} %get-tuple-element.680) | copy-start | bytes 1572868
  981.7 23.7 %copy-start.61 = (pred[512,1024]{1,0:T(8,128)(4,1)S(1)}, pred[512,1024]{1,0:T(8,128)(4,1)}, u32[]{:S(2)}) copy-start(pred[512,1024]{1,0:T(8,128)(4,1)} %get-tuple-element.681) | copy-start | bytes 1572868
  981.7 23.7 %copy-start.62 = (pred[512,1024]{1,0:T(8,128)(4,1)S(1)}, pred[512,1024]{1,0:T(8,128)(4,1)}, u32[]{:S(2)}) copy-start(pred[512,1024]{1,0:T(8,128)(4,1)} %get-tuple-element.682) | copy-start | bytes 1572868
  981.7 23.7 %copy-start.63 = (pred[512,1024]{1,0:T(8,128)(4,1)S(1)}, pred[512,1024]{1,0:T(8,128)(4,1)}, u32[]{:S(2)}) copy-start(pred[512,1024]{1,0:T(8,128)(4,1)} %get-tuple-element.683) | copy-start | bytes 1572868
  1068.9 28.3 %copy-start.141 = (f32[4]{0:T(128)S(1)}, f32[4]{0:T(128)}, u32[]{:S(2)}) copy-start(f32[4]{0:T(128)} %get-tuple-element.205) | copy-start | bytes 52
  1068.9 28.4 %copy-start.140 = (f32[4]{0:T(128)S(1)}, f32[4]{0:T(128)}, u32[]{:S(2)}) copy-start(f32[4]{0:T(128)} %get-tuple-element.206) | copy-start | bytes 52
  1068.9 28.5 %copy-start.139 = (f32[4]{0:T(128)S(1)}, f32[4]{0:T(128)}, u32[]{:S(2)}) copy-start(f32[4]{0:T(128)} %get-tuple-element.207) | copy-start | bytes 52
  1068.9 28.6 %copy-start.138 = (f32[4]{0:T(128)S(1)}, f32[4]{0:T(128)}, u32[]{:S(2)}) copy-start(f32[4]{0:T(128)} %get-tuple-element.208) | copy-start | bytes 52
  1068.9 28.7 %copy-start.137 = (f32[4]{0:T(128)S(1)}, f32[4]{0:T(128)}, u32[]{:S(2)}) copy-start(f32[4]{0:T(128)} %get-tuple-element.209) | copy-start | bytes 52
  1068.9 28.8 %copy-start.136 = (f32[4]{0:T(128)S(1)}, f32[4]{0:T(128)}, u32[]{:S(2)}) copy-start(f32[4]{0:T(128)} %get-tuple-element.210) | copy-start | bytes 52
  1068.9 28.8 %copy-start.135 = (f32[4]{0:T(128)S(1)}, f32[4]{0:T(128)}, u32[]{:S(2)}) copy-start(f32[4]{0:T(128)} %get-tuple-element.211) | copy-start | bytes 52
  1068.9 28.9 %copy-start.134 = (f32[4]{0:T(128)S(1)}, f32[4]{0:T(128)}, u32[]{:S(2)}) copy-start(f32[4]{0:T(128)} %get-tuple-element.212) | copy-start | bytes 52
  1069.0 29.0 %copy-start.133 = (f32[4]{0:T(128)S(1)}, f32[4]{0:T(128)}, u32[]{:S(2)}) copy-start(f32[4]{0:T(128)} %get-tuple-element.213) | copy-start | bytes 52
  1069.0 29.1 %copy-start.132 = (f32[4]{0:T(128)S(1)}, f32[4]{0:T(128)}, u32[]{:S(2)}) copy-start(f32[4]{0:T(128)} %get-tuple-element.214) | copy-start | bytes 52
  1069.0 29.2 %copy-start.131 = (f32[4]{0:T(128)S(1)}, f32[4]{0:T(128)}, u32[]{:S(2)}) copy-start(f32[4]{0:T(128)} %get-tuple-element.215) | copy-start | bytes 52
  1069.0 43.6 %copy-start.130 = (f32[4]{0:T(128)S(1)}, f32[4]{0:T(128)}, u32[]{:S(2)}) copy-start(f32[4]{0:T(128)} %get-tuple-element.89) | copy-start | bytes 52
  1069.0 43.7 %copy-start.129 = (f32[4]{0:T(128)S(1)}, f32[4]{0:T(128)}, u32[]{:S(2)}) copy-start(f32[4]{0:T(128)} %get-tuple-element.88) | copy-start | bytes 52
  1101.6 184.7 %copy-start.116 = (f32[1,1024]{1,0:T(1,128)S(1)}, f32[1,1024]{1,0:T(1,128)}, u32[]{:S(2)}) copy-start(f32[1,1024]{1,0:T(1,128)} %copy-done.115) | copy-start | bytes 12292
  1101.6 184.7 %copy-start.124 = (f32[256]{0:T(256)S(1)}, f32[256]{0:T(256)}, u32[]{:S(2)}) copy-start(f32[256]{0:T(256)} %copy-done.123) | copy-start | bytes 3076
  1118.6 170.3 %copy-start.126 = (f32[256]{0:T(256)S(1)}, f32[256]{0:T(256)}, u32[]{:S(2)}) copy-start(f32[256]{0:T(256)} %copy-done.125) | copy-start | bytes 3076
  1118.6 170.3 %copy-start.7 = (f32[1,256,1024]{2,1,0:T(8,128)S(1)}, f32[1,256,1024]{2,1,0:T(8,128)}, u32[]{:S(2)}) copy-start(f32[1,256,1024]{2,1,0:T(8,128)} %reduce-scatter.25.cloned.1.call-done) | copy-start | bytes 3145732
  (139 other events, 1740.4 us)
Sparse Core Ops, SparseCore 0:
  10.5 28.5 all-gather.9
  41.2 45.8 all-gather.7
  391.0 77.0 reduce-scatter.20
  470.0 32.1 all-gather.13
  504.3 45.9 all-gather.11
  552.1 24.0 all-gather.15
  577.8 45.9 all-gather.17
  638.4 75.4 reduce-scatter.24
  717.9 46.4 all-gather.19
  767.5 37.1 reduce-scatter.34
  808.1 44.8 reduce-scatter.32
  874.6 32.7 reduce-scatter.30
  910.7 38.4 reduce-scatter.28
  951.4 43.8 reduce-scatter.26
  997.5 43.1 reduce-scatter.22
  1289.0 131.1 reduce-scatter.36
where the time goes:
time: 1440 us; the launch traced here: 1430 us
  waiting for transfers between devices  440 us (31%)
  other arithmetic  384 us (27%)
  matrix products  343 us (24%)
  local copies, waits for them, and re-layouts  217 us (15%)
  blocking collectives  26.3 us (2%)
  between operations  17.7 us (1%)
    reduce_sum x11, other arithmetic, table_sums(): jnp.sum(jnp.where(kind_buckets == number, grad_values, 0.0), axis=(1, 2))  268 us
    dot_general x2, matrix products, masked_scores(): jnp.einsum('qhe,khe->hqk', block_heads, key_heads, preferred_element_type...  243 us
    another operation x198, local copies, waits for them, and re-layouts, table_sums(): kind_sums.append(jnp.stack(number_sums))  150 us
    unnamed x21, waiting for transfers between devices  130 us
    eq x3, other arithmetic, table_bias(): kind_buckets == number  91.3 us
    reduce_scatter x1, waiting for transfers between devices, on_device(): lax.psum_scatter(attention_residual, 'mp', scatter_dimension=1, tiled=True)  76.6 us
    reduce_scatter x1, waiting for transfers between devices, on_device(): lax.psum_scatter(two_term, 'mp', scatter_dimension=1, tiled=True)  75.6 us
    unnamed x392, local copies, waits for them, and re-layouts  51.4 us
  transfers between devices with their start and end apart: 16, of which 8 were waited for; matrix products, arithmetic and copies ran while one was open for 46% of the time, Pallas kernels for 0%

commit v1 on v0

v1 whole, which is shorter than its diff:
```python
import functools
import jax
import jax.numpy as jnp
from jax import lax
from jax.experimental import pallas as pl
from jax.experimental.pallas import tpu as pltpu
from jax.sharding import PartitionSpec as P

NB = 32
thresholds = (12, 16, 23, 32, 46, 64, 91)
BQ = 256
NEG = -1e30
bf16 = jnp.bfloat16
f32 = jnp.float32


def bucket_of(distance):
    magnitude = jnp.abs(distance)
    stepped = 8 + sum(((magnitude >= boundary).astype(jnp.int32) for boundary in thresholds))
    return jnp.where(magnitude < 8, magnitude, stepped) + 16 * (distance > 0).astype(jnp.int32)


def iota(shape, axis):
    return lax.broadcasted_iota(jnp.int32, shape, axis)


def to_bf16(mask):
    return jnp.where(mask, 1.0, 0.0).astype(bf16)


def key_features(labc, tab, k, feats, heads):
    length = labc.shape[0]
    for kind in (0, 1):
        chosen = to_bf16(iota((length, 256), 1) == labc[:, 2 + kind : 3 + kind])
        where_bucket = bucket_of(iota((256, 256), 0) - iota((256, 256), 1))
        for h in range(heads):
            row = tab[(1 + kind) * heads + h : (1 + kind) * heads + h + 1, :]
            wide = jnp.broadcast_to(row, (256, 128))
            toep = jnp.concatenate(
                [
                    jnp.take_along_axis(wide, where_bucket[:, c : c + 128], axis=1)
                    for c in (0, 128)
                ],
                axis=1,
            ).astype(bf16)
            feats[h, :, kind * 256 : kind * 256 + 256] = jnp.dot(
                chosen, toep, preferred_element_type=f32
            ).astype(bf16)
    lane = iota((length, 64), 1)
    mask = jnp.where(
        lane < 8,
        jnp.where(labc[:, 0:1] == lane, 0.0, NEG),
        jnp.where((lane == 8) & (labc[:, 4:5] != 1), NEG, 0.0),
    ).astype(bf16)
    for h in range(heads):
        feats[h, :, 512:576] = k[:, h * 64 : h * 64 + 64]
        feats[h, :, 576:640] = mask


def query_features(labr, first, a):
    def of(row):
        return labr[row : row + 1, pl.ds(first, BQ)]

    sub = iota((256, BQ), 0)
    a[0:256, :] = to_bf16(sub == of(2))
    a[256:512, :] = to_bf16(sub == of(3))
    low = iota((64, BQ), 0)
    a[576:640, :] = jnp.where(
        low < 8, jnp.where(of(0) == low, 1.0, 0.0), jnp.where(low == 8, 1.0, 0.0)
    ).astype(bf16)


def near_buckets(labr, labc, qb, idx, tiles):
    first = pl.multiple_of(qb * BQ, BQ)
    here = labr[1:2, pl.ds(first, BQ)]
    for n in range(4):
        t = 2 * qb - 1 + n

        @pl.when((t >= 0) & (t < tiles))
        def _():
            there = labc[pl.ds(pl.multiple_of(t * 128, 128), 128), 1:2]
            idx[n * 128 : n * 128 + 128, :] = bucket_of(there - here)


def add_near(s_ref, tab, idx, labr, qb, h, own, tiles):
    first = pl.multiple_of(qb * BQ, BQ)
    wide = jnp.broadcast_to(tab[h : h + 1, :], (128, 128))
    padded = labr[4:5, pl.ds(first, BQ)] != 1
    for n in range(4):
        t = 2 * qb - 1 + n

        @pl.when((t >= 0) & (t < tiles))
        def _():
            rows = pl.ds(pl.multiple_of(t * 128, 128), 128)
            got = jnp.concatenate(
                [
                    jnp.take_along_axis(wide, idx[n * 128 : n * 128 + 128, c : c + 128], axis=1)
                    for c in range(0, BQ, 128)
                ],
                axis=1,
            )
            s = s_ref[rows, :] + got
            if n in (1, 2):
                same = iota((128, BQ), 0) + (n - 1) * 128 == iota((128, BQ), 1)
                s = jnp.where(same & padded, own, s)
            s_ref[rows, :] = s


def own_scores(qt, k_block, tab, heads):
    kt = k_block.T.astype(f32)
    prod = qt.astype(f32) * kt
    out = []
    for h in range(heads):
        zero_bias = tab[h, 0] + tab[heads + h, 0] + tab[2 * heads + h, 0]
        out.append(jnp.sum(prod[h * 64 : h * 64 + 64], axis=0, keepdims=True) + zero_bias)
    return out


def far_constant(far, qb, t, h):
    return jnp.where(t < 2 * qb - 1, far[0, h], jnp.where(t > 2 * qb + 2, far[1, h], 0.0))


def rows_max(value):
    return functools.reduce(jnp.maximum, [value[i : i + 8] for i in range(0, value.shape[0], 8)])


def rows_sum(value):
    return functools.reduce(jnp.add, [value[i : i + 8] for i in range(0, value.shape[0], 8)])


def fwd_kernel(heads, far, labr, labc, tab, q, k, v, mixed, ot, lse, feats, a, s_ref, p_ref, vt, idx):
    labr, labc, q, k, v = labr.at[0], labc.at[0], q.at[0], k.at[0], v.at[0]
    mixed, ot, lse = mixed.at[0], ot.at[0], lse.at[0]
    length = labc.shape[0]
    tiles = length // 128
    qb = pl.program_id(1)
    first = pl.multiple_of(qb * BQ, BQ)

    @pl.when(qb == 0)
    def _():
        key_features(labc, tab, k, feats, heads)
        vt[...] = v[...].T

    query_features(labr, first, a)
    near_buckets(labr, labc, qb, idx, tiles)
    qt = q[...].T
    own = own_scores(qt, k[pl.ds(first, BQ), :], tab, heads)
    outs = []
    for h in range(heads):
        a[512:576, :] = qt[h * 64 : h * 64 + 64]
        s_ref[...] = jnp.dot(feats[h], a[...], preferred_element_type=f32)
        add_near(s_ref, tab, idx, labr, qb, h, own[h], tiles)
        top = None
        for t in range(tiles):
            here = rows_max(s_ref[t * 128 : t * 128 + 128, :]) + far_constant(far, qb, t, h)
            top = here if top is None else jnp.maximum(top, here)
        top = jnp.max(top, axis=0, keepdims=True)
        total = jnp.zeros((8, BQ), f32)
        for t in range(tiles):
            shift = top - far_constant(far, qb, t, h)
            p = jnp.exp(s_ref[t * 128 : t * 128 + 128, :] - shift)
            total = total + rows_sum(p)
            p_ref[t * 128 : t * 128 + 128, :] = p.astype(bf16)
        total = jnp.sum(total, axis=0, keepdims=True)
        o = jnp.dot(vt[h * 64 : h * 64 + 64, :], p_ref[...], preferred_element_type=f32)
        o = o * (1.0 / total)
        ot[h * 64 : h * 64 + 64, :] = o
        lse[h : h + 1, :] = top + jnp.log(total)
        outs.append(o)
    mixed[...] = jnp.concatenate(outs, axis=0).T.astype(bf16)


def bwd_kernel(
    heads, far, labr, labc, tab, spread, q, k, v, go, ot, lse,
    dqkv, tg,
    feats, a, s_ref, dp_ref, pd, ends, acc, cxy, cp, sums, idx,
):
    labr, labc, q, k, v = labr.at[0], labc.at[0], q.at[0], k.at[0], v.at[0]
    go, ot, lse, dqkv, tg = go.at[0], ot.at[0], lse.at[0], dqkv.at[0], tg.at[0]
    length = labc.shape[0]
    width = heads * 64
    tiles = length // 128
    qb = pl.program_id(1)
    first = pl.multiple_of(qb * BQ, BQ)

    @pl.when(qb == 0)
    def _():
        key_features(labc, tab, k, feats, heads)
        sub = iota((256, length), 0)
        ends[0:256, :] = to_bf16(sub == labr[2:3, :])
        ends[256:512, :] = to_bf16(sub == labr[3:4, :])
        acc[...] = jnp.zeros_like(acc)
        cxy[...] = jnp.zeros_like(cxy)
        cp[...] = jnp.zeros_like(cp)
        sums[...] = jnp.zeros_like(sums)
        ends[512 : 512 + width, :] = k[...].T

    query_features(labr, first, a)
    near_buckets(labr, labc, qb, idx, tiles)
    qt = q[...].T
    own = own_scores(qt, k[pl.ds(first, BQ), :], tab, heads)
    gt = go[...].T
    delta_all = gt.astype(f32) * ot[...]
    flipped = [
        to_bf16(255 - iota((BQ, 256), 1) == labc[pl.ds(first, BQ), 2 + kind : 3 + kind])
        for kind in (0, 1)
    ]
    zeros = jnp.zeros((BQ, 64), bf16)
    dqts = []
    for h in range(heads):
        cols = slice(h * 64, h * 64 + 64)
        a[512:576, :] = qt[cols]
        s_ref[...] = jnp.dot(feats[h], a[...], preferred_element_type=f32)
        dp_ref[...] = jnp.dot(v[:, cols], gt[cols], preferred_element_type=f32)
        add_near(s_ref, tab, idx, labr, qb, h, own[h], tiles)
        delta = jnp.sum(delta_all[cols], axis=0, keepdims=True)
        low = jnp.zeros((8, BQ), f32)
        high = jnp.zeros((8, BQ), f32)
        for t in range(tiles):
            rows = slice(t * 128, t * 128 + 128)
            shift = lse[h : h + 1, :] - far_constant(far, qb, t, h)
            p = jnp.exp(s_ref[rows, :] - shift)
            ds = p * (dp_ref[rows, :] - delta)
            pd[rows, 0:BQ] = p.astype(bf16)
            pd[rows, BQ : 2 * BQ] = ds.astype(bf16)
            after = (t * 128 - qb * BQ + iota((128, BQ), 0)) > iota((128, BQ), 1)
            high = high + rows_sum(jnp.where(after, ds, 0.0))
            low = low + rows_sum(ds)
        sums[h * 16 : h * 16 + 8, :] += low - high
        sums[h * 16 + 8 : h * 16 + 16, :] += high
        right = jnp.concatenate(
            [
                jnp.concatenate([go[:, cols], zeros], axis=1),
                jnp.concatenate([zeros, q[:, cols]], axis=1),
            ],
            axis=0,
        )
        acc[h] += jnp.dot(pd[...], right, preferred_element_type=f32)
        dst = pd[:, BQ : 2 * BQ]
        dqts.append(
            jnp.dot(ends[512 + h * 64 : 576 + h * 64, :], dst, preferred_element_type=f32)
        )
        placed = jnp.dot(ends[0:512, :], dst, preferred_element_type=f32)
        coarse = placed.astype(bf16)
        fine = (placed - coarse.astype(f32)).astype(bf16)
        for kind in (0, 1):
            part = slice(kind * 256, kind * 256 + 256)
            cxy[h, part, :] += jnp.dot(
                coarse[part], flipped[kind], preferred_element_type=f32
            ) + jnp.dot(fine[part], flipped[kind], preferred_element_type=f32)
        for half in (0, 1):
            start = qb * 2 + half
            base = pl.multiple_of(start * 128, 128)
            lo = jnp.clip(start - 1, 0, tiles - 3)
            window = pl.ds(pl.multiple_of(lo * 128, 128), 384)
            origin = labc[pl.ds(base, 8), 1:2][0:1, 0:1]
            slot = iota((512, 384), 0)
            rel = labr[1:2, window]
            into = to_bf16(slot == rel - origin + 128)
            put = jnp.dot(
                into,
                pd[window, BQ + half * 128 : BQ + half * 128 + 128],
                preferred_element_type=f32,
            ).astype(bf16)
            from_here = to_bf16(255 - iota((128, 256), 1) == labc[pl.ds(base, 128), 1:2] - origin)
            cp[h] += jnp.dot(put, from_here, preferred_element_type=f32)
    dqkv[pl.ds(first, BQ), 0:width] = jnp.concatenate(dqts, axis=0).T.astype(bf16)

    @pl.when(qb == pl.num_programs(1) - 1)
    def _():
        for h in range(0, heads, 2):
            one, two = acc[h], acc[h + 1]
            dqkv[:, width + h * 64 : width + h * 64 + 128] = jnp.concatenate(
                [one[:, 64:], two[:, 64:]], axis=1
            ).astype(bf16)
            dqkv[:, 2 * width + h * 64 : 2 * width + h * 64 + 128] = jnp.concatenate(
                [one[:, :64], two[:, :64]], axis=1
            ).astype(bf16)
        lines = []
        for kind in (0, 1, 2):
            for h in range(heads):
                c = cp[h] if kind == 0 else cxy[h, (kind - 1) * 256 : kind * 256, :]
                c = jnp.concatenate([c, jnp.zeros_like(c)], axis=1)
                c = pltpu.roll(c, 0, 1, stride=1, stride_axis=0)
                lines.append(jnp.sum(c, axis=0, keepdims=True))
        rel = jnp.dot(
            jnp.concatenate(lines[:heads], axis=0),
            spread[0],
            preferred_element_type=f32,
            precision=lax.Precision.HIGHEST,
        )
        box = jnp.dot(
            jnp.concatenate(lines[heads:], axis=0),
            spread[1],
            preferred_element_type=f32,
            precision=lax.Precision.HIGHEST,
        )
        lane = iota((heads, 128), 1)
        low_all = jnp.concatenate([jnp.sum(sums[h * 16 : h * 16 + 8, :]).reshape(1, 1) for h in range(heads)], axis=0)
        high_all = jnp.concatenate([jnp.sum(sums[h * 16 + 8 : h * 16 + 16, :]).reshape(1, 1) for h in range(heads)], axis=0)
        near_low = jnp.sum(jnp.where(lane < 15, rel, 0.0), axis=1, keepdims=True)
        near_high = jnp.sum(jnp.where((lane >= 16) & (lane < 31), rel, 0.0), axis=1, keepdims=True)
        rel = jnp.where(lane == 15, low_all - near_low, rel)
        rel = jnp.where(lane == 31, high_all - near_high, rel)
        tg[...] = jnp.concatenate([rel, box], axis=0)


def spread_tables():
    slot = jnp.arange(512)
    number = jnp.arange(128)
    rel_t = slot - 383
    rel = (bucket_of(rel_t)[:, None] == number[None]) & (jnp.abs(rel_t) < 91)[:, None]
    box = bucket_of(slot - 255)[:, None] == number[None]
    return jnp.stack([rel, box]).astype(f32)


def label_arrays(segments, positions, boxes, pad_mask):
    zero = jnp.zeros_like(segments)
    labr = jnp.stack([segments, positions, boxes[0], boxes[1], pad_mask, zero, zero, zero], axis=1)
    return labr, jnp.swapaxes(labr, 1, 2)


def table_rows(tables):
    kinds, _, heads = tables.shape
    rows = jnp.swapaxes(tables, 1, 2).reshape(kinds * heads, NB).astype(f32)
    far = jnp.stack([tables[0, 15], tables[0, 31]]).astype(f32)
    return jnp.pad(rows, ((0, 0), (0, 128 - NB))), far


def cost(flops, nbytes):
    return pl.CostEstimate(flops=flops, bytes_accessed=nbytes, transcendentals=0)


def attention_forward(qkv, labr, labc, tab, far):
    rows, length, wide = qkv.shape
    width = wide // 3
    heads = width // 64
    steps = length // BQ
    smem = pl.BlockSpec(memory_space=pltpu.SMEM)
    return pl.pallas_call(
        functools.partial(fwd_kernel, heads),
        out_shape=(
            jax.ShapeDtypeStruct((rows, length, width), bf16),
            jax.ShapeDtypeStruct((rows, width, length), f32),
            jax.ShapeDtypeStruct((rows, 8, length), f32),
        ),
        grid=(rows, steps),
        in_specs=[
            smem,
            pl.BlockSpec((1, 8, length), lambda r, i: (r, 0, 0)),
            pl.BlockSpec((1, length, 8), lambda r, i: (r, 0, 0)),
            pl.BlockSpec(tab.shape, lambda r, i: (0, 0)),
            pl.BlockSpec((1, BQ, width), lambda r, i: (r, i, 0)),
            pl.BlockSpec((1, length, width), lambda r, i: (r, 0, 1)),
            pl.BlockSpec((1, length, width), lambda r, i: (r, 0, 2)),
        ],
        out_specs=(
            pl.BlockSpec((1, BQ, width), lambda r, i: (r, i, 0)),
            pl.BlockSpec((1, width, BQ), lambda r, i: (r, 0, i)),
            pl.BlockSpec((1, 8, BQ), lambda r, i: (r, 0, i)),
        ),
        scratch_shapes=[
            pltpu.VMEM((heads, length, 640), bf16),
            pltpu.VMEM((640, BQ), bf16),
            pltpu.VMEM((length, BQ), f32),
            pltpu.VMEM((length, BQ), bf16),
            pltpu.VMEM((width, length), bf16),
            pltpu.VMEM((512, BQ), jnp.int32),
        ],
        compiler_params=pltpu.CompilerParams(vmem_limit_bytes=48 << 20),
        cost_estimate=cost(rows * heads * length * length * 1664, rows * length * wide * 4),
    )(far, labr, labc, tab, qkv, qkv, qkv)


def attention_backward(qkv, labr, labc, tab, far, go, ot, lse):
    rows, length, wide = qkv.shape
    width = wide // 3
    heads = width // 64
    steps = length // BQ
    spread = spread_tables()
    smem = pl.BlockSpec(memory_space=pltpu.SMEM)
    return pl.pallas_call(
        functools.partial(bwd_kernel, heads),
        out_shape=(
            jax.ShapeDtypeStruct((rows, length, wide), bf16),
            jax.ShapeDtypeStruct((rows, 3 * heads, 128), f32),
        ),
        grid=(rows, steps),
        in_specs=[
            smem,
            pl.BlockSpec((1, 8, length), lambda r, i: (r, 0, 0)),
            pl.BlockSpec((1, length, 8), lambda r, i: (r, 0, 0)),
            pl.BlockSpec(tab.shape, lambda r, i: (0, 0)),
            pl.BlockSpec(spread.shape, lambda r, i: (0, 0, 0)),
            pl.BlockSpec((1, BQ, width), lambda r, i: (r, i, 0)),
            pl.BlockSpec((1, length, width), lambda r, i: (r, 0, 1)),
            pl.BlockSpec((1, length, width), lambda r, i: (r, 0, 2)),
            pl.BlockSpec((1, BQ, width), lambda r, i: (r, i, 0)),
            pl.BlockSpec((1, width, BQ), lambda r, i: (r, 0, i)),
            pl.BlockSpec((1, 8, BQ), lambda r, i: (r, 0, i)),
        ],
        out_specs=(
            pl.BlockSpec((1, length, wide), lambda r, i: (r, 0, 0)),
            pl.BlockSpec((1, 3 * heads, 128), lambda r, i: (r, 0, 0)),
        ),
        scratch_shapes=[
            pltpu.VMEM((heads, length, 640), bf16),
            pltpu.VMEM((640, BQ), bf16),
            pltpu.VMEM((length, BQ), f32),
            pltpu.VMEM((length, BQ), f32),
            pltpu.VMEM((length, 2 * BQ), bf16),
            pltpu.VMEM((512 + width, length), bf16),
            pltpu.VMEM((heads, length, 128), f32),
            pltpu.VMEM((heads, 512, 256), f32),
            pltpu.VMEM((heads, 512, 256), f32),
            pltpu.VMEM((heads * 16, BQ), f32),
            pltpu.VMEM((512, BQ), jnp.int32),
        ],
        compiler_params=pltpu.CompilerParams(vmem_limit_bytes=56 << 20),
        cost_estimate=cost(rows * heads * length * length * 5000, rows * length * wide * 6),
    )(far, labr, labc, tab, spread, qkv, qkv, qkv, go, ot, lse)


epsilon = 1e-06
gelu_coefficient = 0.7978845608028654


def rms_scale(row_values, gain_row):
    return (
        row_values
        * lax.rsqrt(jnp.mean(row_values * row_values, axis=-1, keepdims=True) + epsilon)
        * gain_row
    )


def gelu_tanh(values):
    return (
        0.5
        * values
        * (1.0 + jnp.tanh(gelu_coefficient * (values + 0.044715 * values * values * values)))
    )


def gated_unit(gate_rows, up_rows):
    return gelu_tanh(gate_rows) * up_rows


def mm(spec, one, two):
    return jnp.einsum(spec, one, two, preferred_element_type=f32)


def on_device(
    inputs,
    segments,
    positions,
    boxes,
    pad_mask,
    w_qkv,
    w_out,
    w_gate_up,
    w_down,
    bias_tables,
    gains,
    out_grad,
):
    gain_values = gains.astype(f32)
    labr, labc = label_arrays(segments, positions, boxes, pad_mask)
    tab, far = table_rows(bias_tables)

    def over_dp(w, axis):
        return lax.all_gather(w, "dp", axis=axis, tiled=True)

    def rows_of(part):
        return lax.all_gather(part, "mp", axis=1, tiled=True)

    def scatter_rows(whole):
        return lax.psum_scatter(whole, "mp", scatter_dimension=1, tiled=True)

    x = inputs.astype(f32)
    normed_one = rows_of(rms_scale(x, gain_values[0]).astype(bf16))
    wq = over_dp(w_qkv, 1)
    wqkv = jnp.concatenate([wq[0], wq[1], wq[2]], axis=1)
    qkv = mm("rld,dm->rlm", normed_one, wqkv).astype(bf16)
    mixed, ot, lse = attention_forward(qkv, labr, labc, tab, far)
    wo = over_dp(w_out, 1)
    attn = scatter_rows(mm("rlm,md->rld", mixed, wo).astype(bf16)).astype(f32)
    middle = x + attn
    normed_two = rows_of(rms_scale(middle, gain_values[1]).astype(bf16))
    wgu = over_dp(w_gate_up, 1)
    wd = over_dp(w_down, 1)
    og = rows_of(out_grad)
    gate = mm("rld,df->rlf", normed_two, wgu[0])
    up = mm("rld,df->rlf", normed_two, wgu[1])
    hidden, gated_back = jax.vjp(gated_unit, gate, up)
    hidden = hidden.astype(bf16)
    down = scatter_rows(mm("rlf,fd->rld", hidden, wd).astype(bf16)).astype(f32)
    out = (middle + down).astype(bf16)
    hidden_grad = mm("rld,fd->rlf", og, wd)
    gate_grad, up_grad = gated_back(hidden_grad)
    gate_grad, up_grad = gate_grad.astype(bf16), up_grad.astype(bf16)
    n2g = scatter_rows(
        (mm("rlf,df->rld", gate_grad, wgu[0]) + mm("rlf,df->rld", up_grad, wgu[1])).astype(bf16)
    ).astype(f32)
    w_down_grad = mm("rlf,rld->fd", hidden, og)
    w_gate_grad = mm("rld,rlf->df", normed_two, gate_grad)
    w_up_grad = mm("rld,rlf->df", normed_two, up_grad)

    def grads_over_dp(whole, axis):
        return lax.psum_scatter(
            whole.astype(bf16), "dp", scatter_dimension=axis, tiled=True
        ).astype(f32)

    gate_up_out = grads_over_dp(jnp.stack([w_gate_grad, w_up_grad]), 1)
    down_out = grads_over_dp(w_down_grad, 1)
    unused, norm_back_two = jax.vjp(rms_scale, middle, gain_values[1])
    middle_part, gain_two = norm_back_two(n2g)
    middle_grad = middle_part + out_grad.astype(f32)
    attn_grad = rows_of(middle_grad.astype(bf16))
    mixed_grad = mm("rld,md->rlm", attn_grad, wo).astype(bf16)
    w_out_grad = mm("rlm,rld->md", mixed, attn_grad)
    dqkv, tg = attention_backward(qkv, labr, labc, tab, far, mixed_grad, ot, lse)
    width = mixed.shape[2]
    heads = width // 64
    n1g = scatter_rows(mm("rlm,dm->rld", dqkv, wqkv).astype(bf16)).astype(f32)
    w_qkv_grad = mm("rld,rlm->dm", normed_one, dqkv)
    w_qkv_grad = jnp.stack([w_qkv_grad[:, i * width : (i + 1) * width] for i in range(3)])
    qkv_out = grads_over_dp(w_qkv_grad, 1)
    out_out = grads_over_dp(w_out_grad, 1)
    tg = jnp.sum(tg, axis=0)[:, :NB].reshape(3, heads, NB)
    table_out = lax.psum_scatter(
        jnp.swapaxes(tg, 1, 2), "dp", scatter_dimension=1, tiled=True
    )
    unused, norm_back_one = jax.vjp(rms_scale, x, gain_values[0])
    input_part, gain_one = norm_back_one(n1g)
    input_grad = (input_part + middle_grad).astype(bf16)
    gain_out = lax.psum_scatter(
        jnp.stack([gain_one, gain_two]), ("dp", "mp"), scatter_dimension=1, tiled=True
    )
    return (out, input_grad, qkv_out, out_out, gate_up_out, down_out, table_out, gain_out)


def solution(mesh):
    placed = (
        P("dp", "mp", None),
        P("dp", None),
        P("dp", None),
        P(None, "dp", None),
        P("dp", None),
        P(None, "dp", "mp"),
        P("mp", "dp"),
        P(None, "dp", "mp"),
        P("mp", "dp"),
        P(None, None, "mp"),
        P(),
        P("dp", "mp", None),
    )
    return jax.shard_map(
        on_device,
        mesh=mesh,
        in_specs=placed,
        out_specs=(
            P("dp", "mp", None),
            P("dp", "mp", None),
            P(None, "dp", "mp"),
            P("mp", "dp"),
            P(None, "dp", "mp"),
            P("mp", "dp"),
            P(None, "dp", "mp"),
            P(None, ("dp", "mp")),
        ),
        check_vma=False,
    )
```

time: 1440 us -> 844 us (0.59)
  other arithmetic: 384 us -> 23.2 us
  matrix products: 343 us -> 56.7 us
  local copies, waits for them, and re-layouts: 217 us -> 34.5 us
  waiting for transfers between devices: 440 us -> 561 us
  Pallas kernels: 0 us -> 94.1 us
    dot_general x24 -> x15, matrix products: 343 us -> 56.7 us  [mm(): return jnp.einsum(spec, one, two, preferred_element_type=f32)]
    reduce_sum x13 -> x0, other arithmetic: 271 us -> none  [the longest x11 268 us: table_sums(): jnp.sum(jnp.where(kind_buckets == number, grad_values, 0.0), axis=(1, 2))]
    another operation x198 -> x5, local copies, waits for them, and re-layouts: 150 us -> 0.36 us  [the longest x4 0.26 us: label_arrays(): jnp.stack([segments, positions, boxes[0], boxes[1], pad_mask, zero, zero,...]
    pallas_call x0 -> x2, Pallas kernels: none -> 94.1 us  [the longest x1 59.9 us: attention_backward(): pl.pallas_call(functools.partial(bwd_kernel, heads), out_shape=(jax.Shape...]
    eq x4 -> x1, other arithmetic: 91.3 us -> 0.27 us  [spread_tables(): box = bucket_of(slot - 255)[:, None] == number[None]]
    reduce_scatter x4 -> x5, waiting for transfers between devices: 152 us -> 212 us  [the longest x4 172 us: scatter_rows(): return lax.psum_scatter(whole, 'mp', scatter_dimension=1, tiled=True)]
    all_gather x7, waiting for transfers between devices: 157 us -> 201 us  [the longest x4 155 us: rows_of(): return lax.all_gather(part, 'mp', axis=1, tiled=True)]
    unnamed x392 -> x82, local copies, waits for them, and re-layouts: 51.4 us -> 31.6 us
  transfers between devices with their start and end apart: 16 -> 16, of which waited for: 8 -> 15; matrix products, arithmetic and copies ran while one was open for 46% -> 10% of each run, Pallas kernels for 0% -> 7%
where the time goes in v1:
time: 844 us; the launch traced here: 835 us
  waiting for transfers between devices  561 us (66%)
  Pallas kernels  94.1 us (11%)
  matrix products  56.7 us (7%)
  blocking collectives  36 us (4%)
  local copies, waits for them, and re-layouts  34.5 us (4%)
  other arithmetic  23.2 us (3%)
  between operations  15.3 us (2%)
  starting transfers between devices  13.8 us (2%)
    reduce_scatter x4, waiting for transfers between devices, scatter_rows(): return lax.psum_scatter(whole, 'mp', scatter_dimension=1, tiled=True)  172 us
    all_gather x4, waiting for transfers between devices, rows_of(): return lax.all_gather(part, 'mp', axis=1, tiled=True)  155 us
    unnamed x20, waiting for transfers between devices  148 us
    pallas_call x1, Pallas kernels, attention_backward(): pl.pallas_call(functools.partial(bwd_kernel, heads), out_shape=(jax.Shape...  59.9 us
    dot_general x15, matrix products, mm(): return jnp.einsum(spec, one, two, preferred_element_type=f32)  56.7 us
    all_gather x3, waiting for transfers between devices, over_dp(): return lax.all_gather(w, 'dp', axis=axis, tiled=True)  46.1 us
    reduce_scatter x1, waiting for transfers between devices, grads_over_dp(): lax.psum_scatter(whole.astype(bf16), 'dp', scatter_dimension=axis, tiled=...  40.2 us
    pallas_call x1, Pallas kernels, attention_forward(): pl.pallas_call(functools.partial(fwd_kernel, heads), out_shape=(jax.Shape...  34.2 us
  transfers between devices with their start and end apart: 16, of which 15 were waited for; matrix products, arithmetic and copies ran while one was open for 10% of the time, Pallas kernels for 7%

profile of v1, /device:TPU:0, one launch (start us, length us, event | category | flops | bytes accessed | tf_op | source)
XLA Modules:
  0.0 835.0 jit_solution(8692641646479276337)
XLA Ops:
  7.3 0.7 all-gather.10.cloned.1.call-update
  8.0 1.2 fusion.74
  9.2 0.8 fusion.106
  10.0 2.0 fusion.67
  12.7 12.3 %all_gather.26 = bf16[256,1024]{1,0:T(8,128)(2,1)S(1)} all-gather(bf16[256,128]{1,0:T(8,128)(2,1)S(1)} %copy-done.18), channel_id=1, replica_groups=mesh['dp'=8,'mp'=4] {'dp'}, dimensions={1}, use_global_device_ids=true | all-gather | bytes 589824 | tf_op jit(solution)/shard_map/all_gather | solution.py:471
  25.1 13.9 %all-gather.10.cloned.1.call-done = bf16[3,1024,256]{2,1,0:T(8,128)(2,1)} async-done(((bf16[3,128,256]{2,1,0:T(8,128)(2,1)}), bf16[3,1024,256]{2,1,0:T(8,128)(2,1)}) %all-gather.10.cloned.1.call-update) | async-done | bytes 1572880 | tf_op jit(solution)/shard_map/all_gather | solution.py:471
  39.0 1.5 slice_bitcast_fusion.11
  40.5 46.6 %all-gather.8.cloned.1.call-done = bf16[1,1024,1024]{2,1,0:T(8,128)(2,1)} async-done(((bf16[1,256,1024]{2,1,0:T(8,128)(2,1)}), bf16[1,1024,1024]{2,1,0:T(8,128)(2,1)}) %all-gather.8.cloned.1.call-update) | async-done | bytes 2097168 | tf_op jit(solution)/shard_map/all_gather | solution.py:474
  87.2 3.4 fusion.44.q.k.v
  90.6 34.2 %shard_map.179 = (bf16[1,1024,256]{2,1,0:T(8,128)(2,1)S(1)}, f32[1,256,1024]{2,1,0:T(8,128)S(1)}, f32[1,8,1024]{2,1,0:T(8,128)S(1)}) custom-call(f32[2,4]{1,0:T(2,128)S(1)} %maximum_convert_fusion.far, s32[1,8,1024]{2,1,0:T(8,128)S(1)} %stack.65.labr, s32[1,1024,8]{2,1,0:T(8,128)S(1)} %bitcast.130, f32[12,128]{1,0:T(8,128)S(1)} %pad_convert_fusion.tab, ...), custom_call_target="tpu_custom_call" | custom-call | flops 6979321856 | bytes 3145728 | tf_op jit(solution)/shard_map/pallas_call | solution.py:340
  124.8 1.0 copy-done.5
  126.4 2.1 convert_bitcast_fusion.2
  129.2 42.1 %reduce-scatter.19.cloned.1.call-done = bf16[1,256,1024]{2,1,0:T(8,128)(2,1)} async-done(((bf16[1,1024,1024]{2,1,0:T(8,128)(2,1)}), bf16[1,256,1024]{2,1,0:T(8,128)(2,1)}) %reduce-scatter.19.cloned.1.call-update) | async-done | bytes 524304 | tf_op jit(solution)/shard_map/reduce_scatter | solution.py:477
  171.3 1.3 multiply_reduce_fusion
  172.6 2.0 multiply_convert_fusion.2
  175.3 0.7 all-gather.18.cloned.1.call-update
  176.0 13.2 %reduce-scatter.23.cloned.1.call-start = ((), (), s32[]{:S(2)}) async-start(), calls=%async_computation.17 | async-start | bytes 2621440 | tf_op jit(solution)/shard_map/reduce_scatter | solution.py:477
  189.2 15.0 %all-gather.14.cloned.1.call-done = bf16[2,1024,704]{1,2,0:T(8,128)(2,1)} async-done(((bf16[2,128,704]{1,2,0:T(8,128)(2,1)}), bf16[2,1024,704]{1,2,0:T(8,128)(2,1)}) %all-gather.14.cloned.1.call-update) | async-done | bytes 2883600 | tf_op jit(solution)/shard_map/all_gather | solution.py:471
  204.2 48.0 %all-gather.12.cloned.1.call-done = bf16[1,1024,1024]{2,1,0:T(8,128)(2,1)} async-done(((bf16[1,256,1024]{2,1,0:T(8,128)(2,1)}), bf16[1,1024,1024]{2,1,0:T(8,128)(2,1)}) %all-gather.12.cloned.1.call-update) | async-done | bytes 2097168 | tf_op jit(solution)/shard_map/all_gather | solution.py:474
  252.2 5.4 fusion.19
  257.7 3.3 fusion.21
  261.0 17.2 %all-gather.16.cloned.1.call-done = bf16[704,1024]{1,0:T(8,128)(2,1)} async-done(((bf16[704,128]{1,0:T(8,128)(2,1)}), bf16[704,1024]{1,0:T(8,128)(2,1)}) %all-gather.16.cloned.1.call-update) | async-done | bytes 1441808 | tf_op jit(solution)/shard_map/all_gather | solution.py:471
  278.2 47.6 %all-gather.18.cloned.1.call-done = bf16[1,1024,1024]{2,1,0:T(8,128)(2,1)} async-done(((bf16[1,256,1024]{2,1,0:T(8,128)(2,1)}), bf16[1,1024,1024]{2,1,0:T(8,128)(2,1)}) %all-gather.18.cloned.1.call-update) | async-done | bytes 2097168 | tf_op jit(solution)/shard_map/all_gather | solution.py:474
  325.8 9.1 %multiply_convert_fusion = (bf16[1024,704]{0,1:T(8,128)(2,1)S(1)}, bf16[1024,704]{0,1:T(8,128)(2,1)S(1)}, bf16[1024,704]{0,1:T(8,128)(2,1)}) fusion(f32[1024,704]{0,1:T(8,128)} %fusion.21, f32[1024,704]{0,1:T(8,128)} %fusion.19, bf16[704,1024]{1,0:T(8,128)(2,1)} %all-gather.16.cloned.1.call-done, bf16[1,1024,1024]{2,1,0:T(8,128)(2,1)} %all-gather.18.cloned.1.call-done), kind=kOutput, calls=%fused_computation.12 | convolution fusion | flops 1498021888 | bytes 13631488 | tf_op jit(solution)/shard_map/rld,fd->rlf/dot_general | solution.py:449
  334.9 1.8 fusion.59
  336.8 3.2 fusion.6
  340.1 42.7 %reduce-scatter.23.cloned.1.call-done = bf16[1,256,1024]{2,1,0:T(8,128)(2,1)} async-done(((bf16[1,1024,1024]{2,1,0:T(8,128)(2,1)}), bf16[1,256,1024]{2,1,0:T(8,128)(2,1)}) %reduce-scatter.23.cloned.1.call-update) | async-done | bytes 524304 | tf_op jit(solution)/shard_map/reduce_scatter | solution.py:477
  382.8 1.5 fusion.69
  384.3 2.2 fusion.104
  386.6 4.8 fusion.39
  391.4 2.6 copy.39
  394.2 3.9 fusion.47
  398.1 1.7 fusion.50
  399.8 1.8 pad_maximum_fusion
  401.6 8.7 %copy.37 = bf16[2,1024,704]{2,0,1:T(2,128)(2,1)} copy(bf16[2,1024,704]{1,2,0:T(8,128)(2,1)} %pad_maximum_fusion) | data formatting | bytes 5767168
  410.3 7.6 reshape.339
  418.3 0.8 add_convert_fusion.2.spread
  419.2 12.8 %all-gather.20.cloned.1.call-done = bf16[1,1024,1024]{2,1,0:T(8,128)(2,1)} async-done(((bf16[1,256,1024]{2,1,0:T(8,128)(2,1)}), bf16[1,1024,1024]{2,1,0:T(8,128)(2,1)}) %all-gather.20.cloned.1.call-update) | async-done | bytes 2097168 | tf_op jit(solution)/shard_map/all_gather | solution.py:474
  432.0 2.3 fusion.56
  434.3 1.0 copy.35
  435.4 3.1 fusion.64.go
  438.5 59.9 %shard_map.180 = (bf16[1,1024,768]{2,1,0:T(8,128)(2,1)}, f32[1,12,128]{2,1,0:T(8,128)}) custom-call(f32[2,4]{1,0:T(2,128)} %copy-done.3, s32[1,8,1024]{2,1,0:T(8,128)} %copy-done.1, s32[1,1024,8]{2,1,0:T(8,128)} %bitcast.131, f32[12,128]{1,0:T(8,128)} %copy-done.2, f32[2,512,128]{2,1,0:T(8,128)} %add_convert_fusion.2.spread, ...), custom_call_target="tpu_custom_call" | custom-call | flops 20971520000 | bytes 4718592 | tf_op jit(solution)/shard_map/pallas_call | solution.py:382
  498.4 3.3 fusion.30
  501.9 1.4 pad_maximum_fusion.2
  503.8 4.6 convert_bitcast_fusion
  508.5 1.3 copy-done.30
  509.8 4.6 convert_bitcast_fusion.1
  516.3 1.1 copy.40
  517.4 0.8 convert_element_type.267
  518.1 2.5 reduce-scatter.31.cloned.1.call-done
  520.7 1.4 reshape.340
  522.7 0.9 convert_element_type.265
  523.7 23.6 %all-reduce.1 = f32[3,32,4]{2,1,0:T(8,128)S(1)} all-reduce(f32[3,32,4]{2,1,0:T(8,128)S(1)} %bitcast.138), channel_id=10, replica_groups=mesh['dp'=8,'mp'=4] {'dp'}, use_global_device_ids=true, to_apply=%region_12.13.clone | all-reduce | flops 384 | bytes 3072
  548.0 10.1 %reduce-scatter.29.cloned.1.call-done = bf16[128,256]{1,0:T(8,128)(2,1)} async-done(((bf16[1024,256]{1,0:T(8,128)(2,1)}), bf16[128,256]{1,0:T(8,128)(2,1)}) %reduce-scatter.29.cloned.1.call-update) | async-done | bytes 65552
  558.1 0.9 copy.36
  559.7 40.2 %reduce-scatter.27.cloned.1.call-done = bf16[3,128,256]{2,1,0:T(8,128)(2,1)} async-done(((bf16[3,1024,256]{2,1,0:T(8,128)(2,1)}), bf16[3,128,256]{2,1,0:T(8,128)(2,1)}) %reduce-scatter.27.cloned.1.call-update) | async-done | bytes 196624 | tf_op jit(solution)/shard_map/reduce_scatter | solution.py:509
  599.9 1.7 convert_element_type.262
  601.6 44.3 %reduce-scatter.25.cloned.1.call-done = bf16[1,256,1024]{2,1,0:T(8,128)(2,1)} async-done(((bf16[1,1024,1024]{2,1,0:T(8,128)(2,1)}), bf16[1,256,1024]{2,1,0:T(8,128)(2,1)}) %reduce-scatter.25.cloned.1.call-update) | async-done | bytes 524304 | tf_op jit(solution)/shard_map/reduce_scatter | solution.py:477
  645.9 1.6 fusion.70
  647.5 1.0 copy.43
  648.6 42.8 %reduce-scatter.21.cloned.1.call-done = bf16[1,256,1024]{2,1,0:T(8,128)(2,1)} async-done(((bf16[1,1024,1024]{2,1,0:T(8,128)(2,1)}), bf16[1,256,1024]{2,1,0:T(8,128)(2,1)}) %reduce-scatter.21.cloned.1.call-update) | async-done | bytes 524304 | tf_op jit(solution)/shard_map/reduce_scatter | solution.py:477
  691.4 2.8 fusion.73
  694.2 132.7 %reduce-scatter.35.cloned.1.call-done = f32[32,2]{1,0:T(8,128)} async-done(((f32[1024,2]{1,0:T(8,128)}), f32[32,2]{1,0:T(8,128)}) %reduce-scatter.35.cloned.1.call-update) | async-done | bytes 272
  826.9 1.4 copy.44
  (123 shorter events, 7.2 us)
Async XLA Ops:
  7.2 5.0 copy-start.21
  7.2 5.0 copy-start.22
  7.2 5.0 copy-start.23
  7.2 5.0 copy-start.24
  7.2 5.3 copy-start.19
  7.2 5.5 copy-start.18
  7.2 31.8 %all-gather.10.cloned.1.call-start = ((), (), s32[]{:S(2)}) async-start(), calls=%async_computation.10 | async-start | bytes 1769472 | tf_op jit(solution)/shard_map/all_gather | solution.py:471
  8.0 79.2 %all-gather.8.cloned.1.call-start = ((), (), s32[]{:S(2)}) async-start(), calls=%async_computation.9 | async-start | bytes 2621440 | tf_op jit(solution)/shard_map/all_gather | solution.py:474
  12.1 159.2 %reduce-scatter.19.cloned.1.call-start = ((), (), s32[]{:S(2)}) async-start(), calls=%async_computation.11 | async-start | bytes 2621440 | tf_op jit(solution)/shard_map/reduce_scatter | solution.py:477
  12.3 78.3 %copy-start.1 = (s32[1,8,1024]{2,1,0:T(8,128)}, s32[1,8,1024]{2,1,0:T(8,128)S(1)}, u32[]{:S(2)}) copy-start(s32[1,8,1024]{2,1,0:T(8,128)S(1)} %stack.65.labr) | copy-start | bytes 98308
  12.5 78.1 %copy-start = (s32[1,8,1024]{1,2,0:T(8,128)}, s32[1,8,1024]{1,2,0:T(8,128)S(1)}, u32[]{:S(2)}) copy-start(s32[1,8,1024]{1,2,0:T(8,128)S(1)} %copy.33) | copy-start | bytes 98308
  12.7 77.9 %copy-start.3 = (f32[2,4]{1,0:T(2,128)}, f32[2,4]{1,0:T(2,128)S(1)}, u32[]{:S(2)}) copy-start(f32[2,4]{1,0:T(2,128)S(1)} %maximum_convert_fusion.far) | copy-start | bytes 100
  12.7 77.9 %copy-start.2 = (f32[12,128]{1,0:T(8,128)}, f32[12,128]{1,0:T(8,128)S(1)}, u32[]{:S(2)}) copy-start(f32[12,128]{1,0:T(8,128)S(1)} %pad_convert_fusion.tab) | copy-start | bytes 18436
  40.5 50.0 %copy-start.12 = (bf16[1024,256]{1,0:T(8,128)(2,1)}, bf16[1024,256]{1,0:T(8,128)(2,1)S(1)}, u32[]{:S(2)}) copy-start(bf16[1024,256]{1,0:T(8,128)(2,1)S(1)} %get-tuple-element.30) | copy-start | bytes 1572868
  40.5 50.0 %copy-start.14 = (bf16[1024,256]{1,0:T(8,128)(2,1)}, bf16[1024,256]{1,0:T(8,128)(2,1)S(1)}, u32[]{:S(2)}) copy-start(bf16[1024,256]{1,0:T(8,128)(2,1)S(1)} %get-tuple-element.31) | copy-start | bytes 1572868
  40.5 50.0 %copy-start.16 = (bf16[1024,256]{1,0:T(8,128)(2,1)}, bf16[1024,256]{1,0:T(8,128)(2,1)S(1)}, u32[]{:S(2)}) copy-start(bf16[1024,256]{1,0:T(8,128)(2,1)S(1)} %get-tuple-element.32) | copy-start | bytes 1572868
  90.6 34.2 %copy-start.4 = (bf16[1,1024,768]{2,1,0:T(8,128)(2,1)}, bf16[1,1024,768]{2,1,0:T(8,128)(2,1)S(1)}, u32[]{:S(2)}) copy-start(bf16[1,1024,768]{2,1,0:T(8,128)(2,1)S(1)} %fusion.44.q.k.v) | copy-start | bytes 4718596
  124.8 1.0 copy-start.5
  125.8 0.6 copy-start.6
  126.4 44.9 %copy-start.7 = (bf16[1,256,1024]{2,1,0:T(8,128)(2,1)S(1)}, bf16[1,256,1024]{2,1,0:T(8,128)(2,1)}, u32[]{:S(2)}) copy-start(bf16[1,256,1024]{2,1,0:T(8,128)(2,1)} %param.12) | copy-start | bytes 1572868
  128.6 75.6 %all-gather.14.cloned.1.call-start = ((), (), s32[]{:S(2)}) async-start(), calls=%async_computation.13 | async-start | bytes 3244032 | tf_op jit(solution)/shard_map/all_gather | solution.py:471
  129.1 123.1 %all-gather.12.cloned.1.call-start = ((), (), s32[]{:S(2)}) async-start(), calls=%async_computation.12 | async-start | bytes 2621440 | tf_op jit(solution)/shard_map/all_gather | solution.py:474
  174.7 103.5 %all-gather.16.cloned.1.call-start = ((), (), s32[]{:S(2)}) async-start(), calls=%async_computation.14 | async-start | bytes 1622016 | tf_op jit(solution)/shard_map/all_gather | solution.py:471
  175.3 150.5 %all-gather.18.cloned.1.call-start = ((), (), s32[]{:S(2)}) async-start(), calls=%async_computation.16 | async-start | bytes 2621440 | tf_op jit(solution)/shard_map/all_gather | solution.py:474
  176.0 206.7 %reduce-scatter.23.cloned.1.call-start = ((), (), s32[]{:S(2)}) async-start(), calls=%async_computation.17 | async-start | bytes 2621440 | tf_op jit(solution)/shard_map/reduce_scatter | solution.py:477
  252.2 5.4 copy-start.25
  252.2 5.4 copy-start.28
  325.8 9.1 %copy-start.26 = (bf16[2,1024,704]{1,2,0:T(8,128)(2,1)S(1)}, bf16[2,1024,704]{1,2,0:T(8,128)(2,1)}, u32[]{:S(2)}) copy-start(bf16[2,1024,704]{1,2,0:T(8,128)(2,1)} %all-gather.14.cloned.1.call-done) | copy-start | bytes 8650756
  334.9 1.9 copy-start.32
  334.9 1.9 copy-start.33
  340.0 42.8 %copy-start.8 = (bf16[1,256,1024]{2,1,0:T(8,128)(2,1)S(1)}, bf16[1,256,1024]{2,1,0:T(8,128)(2,1)}, u32[]{:S(2)}) copy-start(bf16[1,256,1024]{2,1,0:T(8,128)(2,1)} %reduce-scatter.19.cloned.1.call-done) | copy-start | bytes 1572868
  340.0 44.3 %copy-start.9 = (bf16[1,256,1024]{2,1,0:T(8,128)(2,1)S(1)}, bf16[1,256,1024]{2,1,0:T(8,128)(2,1)}, u32[]{:S(2)}) copy-start(bf16[1,256,1024]{2,1,0:T(8,128)(2,1)} %param.23) | copy-start | bytes 1572868
  340.0 92.0 %all-gather.20.cloned.1.call-start = ((), (), s32[]{:S(2)}) async-start(), calls=%async_computation.18 | async-start | bytes 2621440 | tf_op jit(solution)/shard_map/all_gather | solution.py:474
  386.6 129.7 %reduce-scatter.33.cloned.1.call-start = ((), (), s32[]{:S(2)}) async-start(), calls=%async_computation.23 | async-start | bytes 1769472
  394.1 126.6 %reduce-scatter.31.cloned.1.call-start = ((), (), s32[]{:S(2)}) async-start(), calls=%async_computation.22 | async-start | bytes 3244032
  394.1 3.9 copy-start.29
  394.2 3.9 copy-start.34
  418.0 140.1 %reduce-scatter.29.cloned.1.call-start = ((), (), s32[]{:S(2)}) async-start(), calls=%async_computation.21 | async-start | bytes 589824
  435.3 164.6 %reduce-scatter.27.cloned.1.call-start = ((), (), s32[]{:S(2)}) async-start(), calls=%async_computation.20 | async-start | bytes 1769472 | tf_op jit(solution)/shard_map/reduce_scatter | solution.py:509
  438.5 59.9 %copy-start.27 = (bf16[1,1024,1024]{2,1,0:T(8,128)(2,1)S(1)}, bf16[1,1024,1024]{2,1,0:T(8,128)(2,1)}, u32[]{:S(2)}) copy-start(bf16[1,1024,1024]{2,1,0:T(8,128)(2,1)} %all-gather.8.cloned.1.call-done) | copy-start | bytes 6291460
  501.8 1.5 copy-start.13
  501.8 1.5 copy-start.15
  501.8 1.9 copy-start.17
  503.2 142.7 %reduce-scatter.25.cloned.1.call-start = ((), (), s32[]{:S(2)}) async-start(), calls=%async_computation.19 | async-start | bytes 2621440 | tf_op jit(solution)/shard_map/reduce_scatter | solution.py:477
  508.4 1.4 copy-start.30
  508.4 182.9 %reduce-scatter.21.cloned.1.call-start = ((), (), s32[]{:S(2)}) async-start(), calls=%async_computation.15 | async-start | bytes 2621440 | tf_op jit(solution)/shard_map/reduce_scatter | solution.py:477
  514.4 0.7 copy-start.31
  514.4 9.2 %copy-start.20 = (f32[1,12,128]{2,1,0:T(8,128)S(1)}, f32[1,12,128]{2,1,0:T(8,128)}, u32[]{:S(2)}) copy-start(f32[1,12,128]{2,1,0:T(8,128)} %get-tuple-element.17) | copy-start | bytes 18436
  514.4 312.5 %reduce-scatter.35.cloned.1.call-start = ((), (), s32[]{:S(2)}) async-start(), calls=%async_computation.24 | async-start | bytes 540672
  522.7 168.7 %copy-start.10 = (bf16[1,256,1024]{2,1,0:T(8,128)(2,1)S(1)}, bf16[1,256,1024]{2,1,0:T(8,128)(2,1)}, u32[]{:S(2)}) copy-start(bf16[1,256,1024]{2,1,0:T(8,128)(2,1)} %reduce-scatter.23.cloned.1.call-done) | copy-start | bytes 1572868
  645.9 45.5 %copy-start.11 = (bf16[1,256,1024]{2,1,0:T(8,128)(2,1)S(1)}, bf16[1,256,1024]{2,1,0:T(8,128)(2,1)}, u32[]{:S(2)}) copy-start(bf16[1,256,1024]{2,1,0:T(8,128)(2,1)} %reduce-scatter.25.cloned.1.call-done) | copy-start | bytes 1572868
Sparse Core Ops, SparseCore 0:
  10.0 29.0 all-gather.9
  41.2 45.9 all-gather.7
  128.7 42.5 reduce-scatter.18
  173.2 30.9 all-gather.13
  206.3 45.9 all-gather.11
  254.1 24.0 all-gather.15
  279.8 45.9 all-gather.17
  340.1 42.5 reduce-scatter.22
  386.7 45.2 all-gather.19
  435.1 37.1 reduce-scatter.32
  475.8 44.8 reduce-scatter.30
  523.9 34.1 reduce-scatter.28
  561.4 38.4 reduce-scatter.26
  602.0 43.8 reduce-scatter.24
  648.1 43.1 reduce-scatter.20
  693.5 133.3 reduce-scatter.34

commit v2 on v1

--- a/solution.py
+++ b/solution.py
@@ -421,6 +421,78 @@
     )(far, labr, labc, tab, spread, qkv, qkv, qkv, go, ot, lse)
 
 
+def dot_nt(one, two):
+    return lax.dot_general(one, two, (((1,), (1,)), ((), ())), preferred_element_type=f32)
+
+
+def dot_nn(one, two):
+    return jnp.dot(one, two, preferred_element_type=f32)
+
+
+def ffn_kernel(n2, og, w, down, n2g, dw, n2t, ogt, gate, up, hg, hid, dgate, dup):
+    depth = n2.shape[1]
+    wide = w.shape[3]
+    wg = w[:, 0].reshape(depth, wide)
+    wu = w[:, 1].reshape(depth, wide)
+    wd = w[:, 2].reshape(depth, wide)
+    gate[...] = dot_nn(n2[...], wg)
+    up[...] = dot_nn(n2[...], wu)
+    hg[...] = dot_nn(og[...], wd)
+    n2t[...] = n2[...].T
+    ogt[...] = og[...].T
+
+    def chunk(c, _):
+        rows = pl.ds(pl.multiple_of(c * 16, 16), 16)
+        g, u, back = gate[rows, :], up[rows, :], hg[rows, :]
+        square = g * g
+        t = jnp.tanh(gelu_coefficient * (g + 0.044715 * square * g))
+        half = 0.5 * (1.0 + t)
+        act = g * half
+        slope = half + 0.5 * g * (1.0 - t * t) * (
+            gelu_coefficient * (1.0 + 0.134145 * square)
+        )
+        hid[rows, :] = (act * u).astype(bf16)
+        dgate[rows, :] = (back * u * slope).astype(bf16)
+        dup[rows, :] = (back * act).astype(bf16)
+        return 0
+
+    lax.fori_loop(0, n2.shape[0] // 16, chunk, 0, unroll=2)
+    n2g[...] = dot_nt(dgate[...], wg) + dot_nt(dup[...], wu)
+    down[...] = dot_nt(hid[...], wd)
+    parts = dw.shape[0]
+    dw[:, 0] = dot_nn(n2t[...], dgate[...]).astype(bf16).reshape(parts, -1, wide)
+    dw[:, 1] = dot_nn(n2t[...], dup[...]).astype(bf16).reshape(parts, -1, wide)
+    dw[:, 2] = dot_nn(ogt[...], hid[...]).astype(bf16).reshape(parts, -1, wide)
+
+
+def ffn(n2, og, w):
+    tokens, depth = n2.shape
+    wide = w.shape[3]
+    vmem = pl.BlockSpec(memory_space=pltpu.VMEM)
+    return pl.pallas_call(
+        ffn_kernel,
+        out_shape=(
+            jax.ShapeDtypeStruct((tokens, depth), f32),
+            jax.ShapeDtypeStruct((tokens, depth), f32),
+            jax.ShapeDtypeStruct(w.shape, bf16),
+        ),
+        in_specs=[vmem] * 3,
+        out_specs=(vmem,) * 3,
+        scratch_shapes=[
+            pltpu.VMEM((depth, tokens), bf16),
+            pltpu.VMEM((depth, tokens), bf16),
+            pltpu.VMEM((tokens, wide), f32),
+            pltpu.VMEM((tokens, wide), f32),
+            pltpu.VMEM((tokens, wide), f32),
+            pltpu.VMEM((tokens, wide), bf16),
+            pltpu.VMEM((tokens, wide), bf16),
+            pltpu.VMEM((tokens, wide), bf16),
+        ],
+        compiler_params=pltpu.CompilerParams(vmem_limit_bytes=56 << 20),
+        cost_estimate=cost(18 * tokens * depth * wide, 4 * w.size + 12 * tokens * depth),
+    )(n2, og, w)
+
+
 epsilon = 1e-06
 gelu_coefficient = 0.7978845608028654
 
@@ -433,23 +505,49 @@
     )
 
 
-def gelu_tanh(values):
-    return (
-        0.5
-        * values
-        * (1.0 + jnp.tanh(gelu_coefficient * (values + 0.044715 * values * values * values)))
-    )
-
-
-def gated_unit(gate_rows, up_rows):
-    return gelu_tanh(gate_rows) * up_rows
-
-
 def mm(spec, one, two):
     return jnp.einsum(spec, one, two, preferred_element_type=f32)
 
 
+def bits_of(size):
+    return [1 << b for b in reversed(range(size.bit_length() - 1))]
+
+
+def swap(value, axis, size, distance):
+    return lax.ppermute(value, axis, [(j, j ^ distance) for j in range(size)])
+
+
+def gather_xor(own, axis, size, bits):
+    held = {0: own}
+    for b in bits:
+        held.update({k ^ b: swap(v, axis, size, b) for k, v in list(held.items())})
+    return held
+
+
+def scatter_xor(parts, axis, size, bits):
+    held = dict(parts)
+    for b in reversed(bits):
+        for k in [k for k in held if not k & b]:
+            held[k] = held[k] + swap(held.pop(k | b).astype(bf16), axis, size, b).astype(f32)
+    return held[0]
+
+
+def scatter_dp(whole, size):
+    me = lax.axis_index("dp")
+    b = 1
+    while b < size:
+        pairs = whole.reshape((whole.shape[0] // 2, 2) + whole.shape[1:])
+        mine = (me // b) % 2
+        keep = lax.dynamic_index_in_dim(pairs, mine, 1, keepdims=False)
+        send = lax.dynamic_index_in_dim(pairs, 1 - mine, 1, keepdims=False)
+        whole = keep.astype(f32) + swap(send.astype(bf16), "dp", size, b).astype(f32)
+        b *= 2
+    return whole[0]
+
+
 def on_device(
+    dp,
+    mp,
     inputs,
     segments,
     positions,
@@ -466,76 +564,127 @@
     gain_values = gains.astype(f32)
     labr, labc = label_arrays(segments, positions, boxes, pad_mask)
     tab, far = table_rows(bias_tables)
-
-    def over_dp(w, axis):
-        return lax.all_gather(w, "dp", axis=axis, tiled=True)
-
-    def rows_of(part):
-        return lax.all_gather(part, "mp", axis=1, tiled=True)
-
-    def scatter_rows(whole):
-        return lax.psum_scatter(whole, "mp", scatter_dimension=1, tiled=True)
-
+    here = lax.axis_index("mp")
+    rows, part, depth = inputs.shape
+    width = w_out.shape[0]
+    heads = width // 64
+    slice_rows = w_qkv.shape[1]
+    wide = w_down.shape[0]
+    all_bits = bits_of(mp)
+    near_bit, far_bits = 1, all_bits[:-1]
+
+    def in_order(held):
+        stacked = jnp.stack([held[k] for k in range(mp)])
+        return jnp.concatenate(
+            [lax.dynamic_index_in_dim(stacked, here ^ m, 0, keepdims=False) for m in range(mp)],
+            axis=1,
+        )
+
+    def block_for(whole, k):
+        return lax.dynamic_slice_in_dim(whole, (here ^ k) * part, part, 1)
+
+    def exchange(blocks):
+        return {k: v if k == 0 else swap(v, "mp", mp, k) for k, v in blocks.items()}
+
+    wqkv = lax.all_gather(
+        jnp.swapaxes(w_qkv, 0, 1).reshape(slice_rows, 3 * width), "dp", axis=0, tiled=True
+    )
     x = inputs.astype(f32)
-    normed_one = rows_of(rms_scale(x, gain_values[0]).astype(bf16))
-    wq = over_dp(w_qkv, 1)
-    wqkv = jnp.concatenate([wq[0], wq[1], wq[2]], axis=1)
+    n1 = gather_xor(rms_scale(x, gain_values[0]).astype(bf16), "mp", mp, all_bits)
+    normed_one = in_order(n1)
+    wo_held = gather_xor(w_out.T, "mp", mp, all_bits)
+    wo = lax.all_gather(
+        jnp.concatenate([wo_held[k] for k in range(mp)], axis=1), "dp", axis=0, tiled=True
+    )
+    packed = jnp.concatenate([w_gate_up, w_down.T[None]], axis=0)
+    packs = gather_xor(packed, "mp", mp, far_bits)
+    ffn_w = {
+        k: lax.all_gather(v.reshape(3 * slice_rows, wide), "dp", axis=0, tiled=True).reshape(
+            dp, 3, slice_rows, wide
+        )
+        for k, v in packs.items()
+    }
+
     qkv = mm("rld,dm->rlm", normed_one, wqkv).astype(bf16)
     mixed, ot, lse = attention_forward(qkv, labr, labc, tab, far)
-    wo = over_dp(w_out, 1)
-    attn = scatter_rows(mm("rlm,md->rld", mixed, wo).astype(bf16)).astype(f32)
+    mixed_in = exchange({k: block_for(mixed, k) for k in range(mp)})
+    mixed_all = jnp.concatenate([mixed_in[k] for k in range(mp)], axis=2)
+    attn = mm("rlm,dm->rld", mixed_all, wo)
     middle = x + attn
-    normed_two = rows_of(rms_scale(middle, gain_values[1]).astype(bf16))
-    wgu = over_dp(w_gate_up, 1)
-    wd = over_dp(w_down, 1)
-    og = rows_of(out_grad)
-    gate = mm("rld,df->rlf", normed_two, wgu[0])
-    up = mm("rld,df->rlf", normed_two, wgu[1])
-    hidden, gated_back = jax.vjp(gated_unit, gate, up)
-    hidden = hidden.astype(bf16)
-    down = scatter_rows(mm("rlf,fd->rld", hidden, wd).astype(bf16)).astype(f32)
-    out = (middle + down).astype(bf16)
-    hidden_grad = mm("rld,fd->rlf", og, wd)
-    gate_grad, up_grad = gated_back(hidden_grad)
-    gate_grad, up_grad = gate_grad.astype(bf16), up_grad.astype(bf16)
-    n2g = scatter_rows(
-        (mm("rlf,df->rld", gate_grad, wgu[0]) + mm("rlf,df->rld", up_grad, wgu[1])).astype(bf16)
-    ).astype(f32)
-    w_down_grad = mm("rlf,rld->fd", hidden, og)
-    w_gate_grad = mm("rld,rlf->df", normed_two, gate_grad)
-    w_up_grad = mm("rld,rlf->df", normed_two, up_grad)
-
-    def grads_over_dp(whole, axis):
-        return lax.psum_scatter(
-            whole.astype(bf16), "dp", scatter_dimension=axis, tiled=True
+
+    normed_two = rms_scale(middle, gain_values[1]).astype(bf16)
+
+    def beside(own):
+        return jnp.concatenate([own, swap(own, "mp", mp, near_bit)], axis=1).reshape(-1, depth)
+
+    n2 = beside(normed_two)
+    og = beside(out_grad)
+    down, n2g, w_grads = None, None, {}
+    for k, w in ffn_w.items():
+        down_k, n2g_k, w_grads[k] = ffn(n2, og, w)
+        down = down_k if down is None else down + down_k
+        n2g = n2g_k if n2g is None else n2g + n2g_k
+
+    def own_sum(both):
+        both = both.reshape(rows, 2 * part, depth)
+        return both[:, :part] + swap(both[:, part:].astype(bf16), "mp", mp, near_bit).astype(f32)
+
+    n2g = own_sum(n2g)
+    out = (middle + own_sum(down)).astype(bf16)
+    unused, norm_back_two = jax.vjp(lambda v: rms_scale(v, gain_values[1]), middle)
+    middle_grad = norm_back_two(n2g)[0] + out_grad.astype(f32)
+    attn_grad = middle_grad.astype(bf16)
+
+    own_terms = {
+        k: lax.psum_scatter(
+            g.reshape(dp * 3 * slice_rows, wide), "dp", scatter_dimension=0, tiled=True
         ).astype(f32)
-
-    gate_up_out = grads_over_dp(jnp.stack([w_gate_grad, w_up_grad]), 1)
-    down_out = grads_over_dp(w_down_grad, 1)
-    unused, norm_back_two = jax.vjp(rms_scale, middle, gain_values[1])
-    middle_part, gain_two = norm_back_two(n2g)
-    middle_grad = middle_part + out_grad.astype(f32)
-    attn_grad = rows_of(middle_grad.astype(bf16))
-    mixed_grad = mm("rld,md->rlm", attn_grad, wo).astype(bf16)
-    w_out_grad = mm("rlm,rld->md", mixed, attn_grad)
-    dqkv, tg = attention_backward(qkv, labr, labc, tab, far, mixed_grad, ot, lse)
-    width = mixed.shape[2]
-    heads = width // 64
-    n1g = scatter_rows(mm("rlm,dm->rld", dqkv, wqkv).astype(bf16)).astype(f32)
-    w_qkv_grad = mm("rld,rlm->dm", normed_one, dqkv)
-    w_qkv_grad = jnp.stack([w_qkv_grad[:, i * width : (i + 1) * width] for i in range(3)])
-    qkv_out = grads_over_dp(w_qkv_grad, 1)
-    out_out = grads_over_dp(w_out_grad, 1)
-    tg = jnp.sum(tg, axis=0)[:, :NB].reshape(3, heads, NB)
-    table_out = lax.psum_scatter(
-        jnp.swapaxes(tg, 1, 2), "dp", scatter_dimension=1, tiled=True
+        for k, g in w_grads.items()
+    }
+    w_grad = scatter_xor(own_terms, "mp", mp, far_bits).reshape(3, slice_rows, wide)
+    gate_up_out = w_grad[:2]
+    down_out = w_grad[2].T
+
+    mixed_grad = mm("rld,dm->rlm", attn_grad, wo).astype(bf16)
+    go = in_order(
+        exchange({k: mixed_grad[:, :, k * width : (k + 1) * width] for k in range(mp)})
     )
-    unused, norm_back_one = jax.vjp(rms_scale, x, gain_values[0])
-    input_part, gain_one = norm_back_one(n1g)
-    input_grad = (input_part + middle_grad).astype(bf16)
-    gain_out = lax.psum_scatter(
-        jnp.stack([gain_one, gain_two]), ("dp", "mp"), scatter_dimension=1, tiled=True
+    dqkv, tg = attention_backward(qkv, labr, labc, tab, far, go, ot, lse)
+    n1g_all = mm("rlm,dm->rld", dqkv, wqkv)
+    n1g = scatter_xor({k: block_for(n1g_all, k) for k in range(mp)}, "mp", mp, all_bits)
+    qkv_term = mm("rld,rlm->dm", normed_one, dqkv)
+    qkv_sum = scatter_dp(qkv_term.reshape(dp, slice_rows, 3 * width), dp)
+    qkv_out = jnp.swapaxes(qkv_sum.reshape(slice_rows, 3, width), 0, 1)
+    out_term = mm("rld,rlm->dm", attn_grad, mixed_all)
+    out_sum = scatter_dp(out_term.reshape(dp, slice_rows, mp * width), dp)
+    out_out = scatter_xor(
+        {k: out_sum[:, k * width : (k + 1) * width] for k in range(mp)}, "mp", mp, all_bits
+    ).T
+    tg = jnp.sum(tg, axis=0)[:, :NB].reshape(3 * heads, dp, NB // dp)
+    table_sum = scatter_dp(jnp.swapaxes(tg, 0, 1), dp)
+    table_out = jnp.swapaxes(table_sum.reshape(3, heads, NB // dp), 1, 2)
+    unused, norm_back_one = jax.vjp(lambda v: rms_scale(v, gain_values[0]), x)
+    input_grad = (norm_back_one(n1g)[0] + middle_grad).astype(bf16)
+
+    own_gains = lax.dynamic_slice_in_dim(
+        gain_values, lax.axis_index("dp") * slice_rows, slice_rows, 1
     )
+    products = (
+        jnp.stack(
+            [
+                jnp.sum(qkv_out * w_qkv.astype(f32), axis=(0, 2)),
+                jnp.sum(gate_up_out * w_gate_up.astype(f32), axis=(0, 2)),
+            ]
+        )
+        / own_gains
+    ).reshape(2, mp, slice_rows // mp)
+    held = {
+        k: lax.dynamic_index_in_dim(products, here ^ k, 1, keepdims=False) for k in range(mp)
+    }
+    for b in reversed(all_bits):
+        for k in [k for k in held if not k & b]:
+            held[k] = held[k] + swap(held.pop(k | b), "mp", mp, b)
+    gain_out = held[0]
     return (out, input_grad, qkv_out, out_out, gate_up_out, down_out, table_out, gain_out)
 
 
@@ -555,7 +704,7 @@
         P("dp", "mp", None),
     )
     return jax.shard_map(
-        on_device,
+        functools.partial(on_device, mesh.shape["dp"], mesh.shape["mp"]),
         mesh=mesh,
         in_specs=placed,
         out_specs=(

time: 844 us -> 429 us (0.51)
  waiting for transfers between devices: 561 us -> 142 us
  matrix products: 56.7 us -> 15.1 us
  blocking collectives: 36 us -> 0 us
  starting transfers between devices: 13.8 us -> 48.9 us
  Pallas kernels: 94.1 us -> 124 us
  local copies, waits for them, and re-layouts: 34.5 us -> 45.1 us
  other arithmetic: 23.2 us -> 33.8 us
    reduce_scatter x5 -> x0, waiting for transfers between devices: 212 us -> none  [the longest x4 172 us: scatter_rows(): return lax.psum_scatter(whole, 'mp', scatter_dimension=1, tiled=True)]
    all_gather x7 -> x4, waiting for transfers between devices: 201 us -> 0.03 us  [the longest x1 0.02 us: on_device(): lax.all_gather(jnp.swapaxes(w_qkv, 0, 1).reshape(slice_rows, 3 * width),...]
    unnamed x20 -> x8, waiting for transfers between devices: 148 us -> 0.12 us
    ppermute x0 -> x36, waiting for transfers between devices: none -> 142 us  [swap(): return lax.ppermute(value, axis, [(j, j ^ distance) for j in range(size)])]
    ppermute x0 -> x36, starting transfers between devices: none -> 48.7 us  [swap(): return lax.ppermute(value, axis, [(j, j ^ distance) for j in range(size)])]
    dot_general x15 -> x6, matrix products: 56.7 us -> 15.1 us  [mm(): return jnp.einsum(spec, one, two, preferred_element_type=f32)]
    pallas_call x0 -> x2, Pallas kernels: none -> 29.5 us  [ffn(): pl.pallas_call(ffn_kernel, out_shape=(jax.ShapeDtypeStruct((tokens, depth...]
    unnamed x1 -> x0, blocking collectives: 23.6 us -> none
  transfers between devices with their start and end apart: 16 -> 42, of which waited for: 15 -> 21; matrix products, arithmetic and copies ran while one was open for 10% -> 20% of each run, Pallas kernels for 7% -> 29%
where the time goes in v2:
time: 429 us; the launch traced here: 424 us
  waiting for transfers between devices  142 us (33%)
  Pallas kernels  124 us (29%)
  starting transfers between devices  48.9 us (11%)
  local copies, waits for them, and re-layouts  45.1 us (11%)
  other arithmetic  33.8 us (8%)
  between operations  15.4 us (4%)
  matrix products  15.1 us (4%)
    ppermute x36, waiting for transfers between devices, swap(): return lax.ppermute(value, axis, [(j, j ^ distance) for j in range(size)])  142 us
    pallas_call x1, Pallas kernels, attention_backward(): pl.pallas_call(functools.partial(bwd_kernel, heads), out_shape=(jax.Shape...  60 us
    ppermute x36, starting transfers between devices, swap(): return lax.ppermute(value, axis, [(j, j ^ distance) for j in range(size)])  48.7 us
    pallas_call x1, Pallas kernels, attention_forward(): pl.pallas_call(functools.partial(fwd_kernel, heads), out_shape=(jax.Shape...  34.4 us
    pallas_call x2, Pallas kernels, ffn(): pl.pallas_call(ffn_kernel, out_shape=(jax.ShapeDtypeStruct((tokens, depth...  29.5 us
    unnamed x109, local copies, waits for them, and re-layouts  18 us
    dot_general x6, matrix products, mm(): return jnp.einsum(spec, one, two, preferred_element_type=f32)  15.1 us
  transfers between devices with their start and end apart: 42, of which 21 were waited for; matrix products, arithmetic and copies ran while one was open for 20% of the time, Pallas kernels for 29%

profile of v2, /device:TPU:0, one launch (start us, length us, event | category | flops | bytes accessed | tf_op | source)
XLA Modules:
  0.0 424.2 jit_solution(1662696091492422185)
XLA Ops:
  7.2 1.8 copy.74
  9.0 4.1 collective-permute-start.7
  13.1 1.6 collective-permute-start.6
  14.7 1.7 collective-permute-done.7
  16.4 1.4 collective-permute-start.8
  17.8 2.9 collective-permute-done.8
  20.7 1.6 pad_maximum_fusion.7
  23.5 2.7 collective-permute-start.11
  26.2 22.7 %collective-permute-done.11 = bf16[3,128,704]{1,2,0:T(8,128)(2,1)S(1)} collective-permute-done((bf16[3,128,704]{1,2,0:T(8,128)(2,1)S(1)}, bf16[3,128,704]{1,2,0:T(8,128)(2,1)S(1)}, u32[]{:S(2)}, u32[]{:S(2)}) %collective-permute-start.11) | collective-permute-done | bytes 540704 | tf_op jit(solution)/shard_map/ppermute | solution.py:517
  52.3 4.1 collective-permute-start
  56.3 20.7 %collective-permute-done.1 = bf16[1,256,1024]{2,1,0:T(8,128)(2,1)S(1)} collective-permute-done((bf16[1,256,1024]{2,1,0:T(8,128)(2,1)S(1)}, bf16[1,256,1024]{2,1,0:T(8,128)(2,1)S(1)}, u32[]{:S(2)}, u32[]{:S(2)}) %collective-permute-start.1) | collective-permute-done | bytes 524320 | tf_op jit(solution)/shard_map/ppermute | solution.py:517
  77.9 10.8 %collective-permute-done.2 = bf16[1,256,1024]{2,1,0:T(8,128)(2,1)S(1)} collective-permute-done((bf16[1,256,1024]{2,1,0:T(8,128)(2,1)S(1)}, bf16[1,256,1024]{2,1,0:T(8,128)(2,1)S(1)}, u32[]{:S(2)}, u32[]{:S(2)}) %collective-permute-start.2) | collective-permute-done | bytes 524320 | tf_op jit(solution)/shard_map/ppermute | solution.py:517
  89.2 3.9 fusion.9.q.k.v
  93.3 34.4 %shard_map.179 = (bf16[1,1024,256]{2,1,0:T(8,128)(2,1)S(1)}, f32[1,256,1024]{2,1,0:T(8,128)S(1)}, f32[1,8,1024]{2,1,0:T(8,128)S(1)}) custom-call(f32[2,4]{1,0:T(2,128)S(1)} %maximum_convert_fusion.far, s32[1,8,1024]{2,1,0:T(8,128)S(1)} %stack.67.labr, s32[1,1024,8]{2,1,0:T(8,128)S(1)} %bitcast.204, f32[12,128]{1,0:T(8,128)S(1)} %pad_convert_fusion.tab, ...), custom_call_target="tpu_custom_call" | custom-call | flops 6979321856 | bytes 3145728 | tf_op jit(solution)/shard_map/pallas_call | solution.py:340
  129.3 3.5 collective-permute-start.5
  134.9 2.7 collective-permute-done.5
  137.6 5.8 %collective-permute-done.4 = bf16[1,256,256]{2,1,0:T(8,128)(2,1)S(1)} collective-permute-done((bf16[1,256,256]{2,1,0:T(8,128)(2,1)S(1)}, bf16[1,256,256]{2,1,0:T(8,128)(2,1)S(1)}, u32[]{:S(2)}, u32[]{:S(2)}) %collective-permute-start.4) | collective-permute-done | bytes 131104 | tf_op jit(solution)/shard_map/ppermute | solution.py:517
  143.4 2.5 multiply_reduce_fusion.1
  147.1 1.6 collective-permute-start.9
  148.6 5.3 %collective-permute-done.10 = bf16[1,256,1024]{2,1,0:T(8,128)(2,1)S(1)} collective-permute-done((bf16[1,256,1024]{2,1,0:T(8,128)(2,1)S(1)}, bf16[1,256,1024]{2,1,0:T(8,128)(2,1)S(1)}, u32[]{:S(2)}, u32[]{:S(2)}) %collective-permute-start.10) | collective-permute-done | bytes 524320 | tf_op jit(solution)/shard_map/ppermute | solution.py:517
  155.0 9.0 %collective-permute-done.9 = bf16[1,256,1024]{2,1,0:T(8,128)(2,1)S(1)} collective-permute-done((bf16[1,256,1024]{2,1,0:T(8,128)(2,1)S(1)}, bf16[1,256,1024]{2,1,0:T(8,128)(2,1)S(1)}, u32[]{:S(2)}, u32[]{:S(2)}) %collective-permute-start.9) | collective-permute-done | bytes 524320 | tf_op jit(solution)/shard_map/ppermute | solution.py:517
  165.0 14.8 %shard_map.181 = (f32[512,1024]{1,0:T(8,128)}, f32[512,1024]{1,0:T(8,128)}, bf16[8,3,128,704]{3,2,1,0:T(8,128)(2,1)}) custom-call(bf16[512,1024]{1,0:T(8,128)(2,1)} %maximum_bitcast_fusion.n2, bf16[512,1024]{1,0:T(8,128)(2,1)} %maximum_bitcast_fusion.1.og, bf16[8,3,128,704]{3,2,1,0:T(8,128)(2,1)} %bitcast.259), custom_call_target="tpu_custom_call" | custom-call | flops 6643777536 | bytes 14942208 | tf_op jit(solution)/shard_map/pallas_call | solution.py:472
  181.8 14.6 %shard_map.180 = (f32[512,1024]{1,0:T(8,128)}, f32[512,1024]{1,0:T(8,128)}, bf16[8,3,128,704]{3,2,1,0:T(8,128)(2,1)}) custom-call(bf16[512,1024]{1,0:T(8,128)(2,1)} %maximum_bitcast_fusion.n2, bf16[512,1024]{1,0:T(8,128)(2,1)} %maximum_bitcast_fusion.1.og, bf16[8,3,128,704]{3,2,1,0:T(8,128)(2,1)} %bitcast.258), custom_call_target="tpu_custom_call" | custom-call | flops 6643777536 | bytes 14942208 | tf_op jit(solution)/shard_map/pallas_call | solution.py:472
  196.5 2.1 add_bitcast_fusion
  199.5 1.7 collective-permute-start.13
  204.2 1.5 fusion.32
  205.6 4.0 copy.81
  209.7 4.9 %collective-permute-done.13 = bf16[1,256,1024]{2,1,0:T(8,128)(2,1)S(1)} collective-permute-done((bf16[1,256,1024]{2,1,0:T(8,128)(2,1)}, bf16[1,256,1024]{2,1,0:T(8,128)(2,1)S(1)}, u32[]{:S(2)}, u32[]{:S(2)}) %collective-permute-start.13) | collective-permute-done | bytes 524320 | tf_op jit(solution)/shard_map/ppermute | solution.py:517
  214.5 1.5 multiply_reduce_fusion
  216.0 7.8 %collective-permute-done.12 = bf16[1,256,1024]{2,1,0:T(8,128)(2,1)} collective-permute-done((bf16[1,256,1024]{2,1,0:T(8,128)(2,1)}, bf16[1,256,1024]{2,1,0:T(8,128)(2,1)}, u32[]{:S(2)}, u32[]{:S(2)}) %collective-permute-start.12) | collective-permute-done | bytes 524320 | tf_op jit(solution)/shard_map/ppermute | solution.py:517
  223.8 3.3 convert_bitcast_fusion.4
  228.4 2.7 fusion.12
  231.1 4.2 collective-permute-start.16
  237.9 1.6 collective-permute-done.16
  239.5 5.3 %collective-permute-done.15 = bf16[1,256,256]{2,1,0:T(8,128)(2,1)S(1)} collective-permute-done((bf16[1,256,256]{2,1,0:T(8,128)(2,1)S(1)}, bf16[1,256,256]{2,1,0:T(8,128)(2,1)S(1)}, u32[]{:S(2)}, u32[]{:S(2)}) %collective-permute-start.15) | collective-permute-done | bytes 131104 | tf_op jit(solution)/shard_map/ppermute | solution.py:517
  245.8 60.0 %shard_map.182 = (bf16[1,1024,768]{2,1,0:T(8,128)(2,1)}, f32[1,12,128]{2,1,0:T(8,128)}) custom-call(f32[2,4]{1,0:T(2,128)} %copy-done.3, s32[1,8,1024]{2,1,0:T(8,128)} %copy-done.1, s32[1,1024,8]{2,1,0:T(8,128)} %bitcast.205, f32[12,128]{1,0:T(8,128)} %copy-done.2, f32[2,512,128]{2,1,0:T(8,128)} %add_convert_fusion.spread, bf16[1,1024,768]{2,1,0:T(8,128)(2,1)} %copy-done.4, ...), custom_call_target="tpu_custom_call" | custom-call | flops 20971520000 | bytes 4718592 | tf_op jit(solution)/shard_map/pallas_call | solution.py:382
  306.6 3.3 fusion.5
  310.0 1.6 copy-done.31
  312.6 1.9 fusion.7
  317.1 1.6 copy.77
  318.7 2.0 copy.106
  321.8 1.6 collective-permute-start.31
  323.4 2.0 collective-permute-start.17
  329.8 8.7 %collective-permute-done.18 = bf16[1,256,1024]{2,1,0:T(8,128)(2,1)S(1)} collective-permute-done((bf16[1,256,1024]{2,1,0:T(8,128)(2,1)}, bf16[1,256,1024]{2,1,0:T(8,128)(2,1)S(1)}, u32[]{:S(2)}, u32[]{:S(2)}) %collective-permute-start.18) | collective-permute-done | bytes 524320 | tf_op jit(solution)/shard_map/ppermute | solution.py:517
  338.4 2.2 fusion.24
  341.8 1.8 bitcast_add_fusion.1
  344.6 2.3 copy.82
  348.3 2.2 bitcast_add_fusion
  352.0 1.3 copy.85
  354.9 1.7 collective-permute-start.24
  356.6 8.0 %collective-permute-done.19 = bf16[1,256,1024]{2,1,0:T(8,128)(2,1)} collective-permute-done((bf16[1,256,1024]{2,1,0:T(8,128)(2,1)}, bf16[1,256,1024]{2,1,0:T(8,128)(2,1)}, u32[]{:S(2)}, u32[]{:S(2)}) %collective-permute-start.19) | collective-permute-done | bytes 524320 | tf_op jit(solution)/shard_map/ppermute | solution.py:517
  364.6 1.5 fusion.19
  369.6 2.4 fusion.15
  372.0 2.4 collective-permute-done.22
  374.5 2.8 collective-permute-done.25
  377.4 1.5 copy.105
  379.6 2.0 collective-permute-start.27
  382.7 8.4 %collective-permute-done.27 = bf16[128,256]{0,1:T(8,128)(2,1)S(1)} collective-permute-done((bf16[128,256]{0,1:T(8,128)(2,1)S(1)}, bf16[128,256]{0,1:T(8,128)(2,1)S(1)}, u32[]{:S(2)}, u32[]{:S(2)}) %collective-permute-start.27) | collective-permute-done | bytes 65568 | tf_op jit(solution)/shard_map/ppermute | solution.py:517
  391.1 4.6 %collective-permute-start.28 = (bf16[128,256]{0,1:T(8,128)(2,1)S(1)}, bf16[128,256]{0,1:T(8,128)(2,1)S(1)}, u32[]{:S(2)}, u32[]{:S(2)}) collective-permute-start(bf16[128,256]{0,1:T(8,128)(2,1)S(1)} %fusion.35), channel_id=1, source_target_pairs={{0,2},{1,3},{2,0},{3,1},{4,6},{5,7},{6,4},{7,5},{8,10},{9,11},{10,... | collective-permute-start | bytes 196616 | tf_op jit(solution)/shard_map/ppermute | solution.py:517
  397.0 7.2 %collective-permute-done.29 = bf16[384,704]{0,1:T(8,128)(2,1)S(1)} collective-permute-done((bf16[384,704]{0,1:T(8,128)(2,1)S(1)}, bf16[384,704]{0,1:T(8,128)(2,1)S(1)}, u32[]{:S(2)}, u32[]{:S(2)}) %collective-permute-start.29) | collective-permute-done | bytes 540704 | tf_op jit(solution)/shard_map/ppermute | solution.py:517
  405.7 1.9 multiply_reduce_fusion.2
  408.5 1.6 fusion.37
  410.1 2.0 collective-permute-start.33
  414.2 2.3 collective-permute-done.35
  (237 shorter events, 51.5 us)
Async XLA Ops:
  7.2 82.1 %all-gather.5.cloned.1.call-start = ((), (), s32[]{:S(2)}) async-start(), calls=%async_computation.2 | async-start | bytes 1769472 | tf_op jit(solution)/shard_map/all_gather | solution.py:589
  9.0 134.4 %all-gather.7.cloned.1.call-start = ((), (), s32[]{:S(2)}) async-start(), calls=%async_computation.3 | async-start | bytes 2359296 | tf_op jit(solution)/shard_map/all_gather | solution.py:596
  9.0 7.4 %collective-permute-start.7 = (bf16[128,256]{0,1:T(8,128)(2,1)}, bf16[128,256]{0,1:T(8,128)(2,1)S(1)}, u32[]{:S(2)}, u32[]{:S(2)}) collective-permute-start(bf16[128,256]{0,1:T(8,128)(2,1)} %bitcast.234), channel_id=1, source_target_pairs={{0,2},{1,3},{2,0},{3,1},{4,6},{5,7},{6,4},{7,5},{8,10},{9,11},{10,... | collective-permute-start | bytes 196616 | tf_op jit(solution)/shard_map/ppermute | solution.py:517
  13.1 4.6 %collective-permute-start.6 = (bf16[128,256]{0,1:T(8,128)(2,1)}, bf16[128,256]{0,1:T(8,128)(2,1)S(1)}, u32[]{:S(2)}, u32[]{:S(2)}) collective-permute-start(bf16[128,256]{0,1:T(8,128)(2,1)} %bitcast.235), channel_id=1, source_target_pairs={{0,1},{1,0},{2,3},{3,2},{4,5},{5,4},{6,7},{7,6},{8,9},{9,8},{10,11... | collective-permute-start | bytes 196616 | tf_op jit(solution)/shard_map/ppermute | solution.py:517
  16.4 4.3 %collective-permute-start.8 = (bf16[128,256]{0,1:T(8,128)(2,1)S(1)}, bf16[128,256]{0,1:T(8,128)(2,1)S(1)}, u32[]{:S(2)}, u32[]{:S(2)}) collective-permute-start(bf16[128,256]{0,1:T(8,128)(2,1)S(1)} %collective-permute-done.7), channel_id=1, source_target_pairs={{0,1},{1,0},{2,3},{3,2},{4,5},{5,4},{6,7},{7,6},{8,9},{9,8},{10,11... | collective-permute-start | bytes 196616 | tf_op jit(solution)/shard_map/ppermute | solution.py:517
  22.3 142.8 %all-gather.11.cloned.1.call-start = ((), (), s32[]{:S(2)}) async-start(), calls=%async_computation.5 | async-start | bytes 5308416 | tf_op jit(solution)/shard_map/all_gather | solution.py:602
  22.3 28.9 %copy-start.7 = (bf16[1,256,1024]{2,1,0:T(8,128)(2,1)S(1)}, bf16[1,256,1024]{2,1,0:T(8,128)(2,1)}, u32[]{:S(2)}) copy-start(bf16[1,256,1024]{2,1,0:T(8,128)(2,1)} %param.12) | copy-start | bytes 1572868
  23.5 27.9 %copy-start.36 = (bf16[2,1024]{1,0:T(2,128)(2,1)S(1)}, bf16[2,1024]{1,0:T(2,128)(2,1)}, u32[]{:S(2)}) copy-start(bf16[2,1024]{1,0:T(2,128)(2,1)} %param.22) | copy-start | bytes 12292
  23.5 25.4 %collective-permute-start.11 = (bf16[3,128,704]{1,2,0:T(8,128)(2,1)S(1)}, bf16[3,128,704]{1,2,0:T(8,128)(2,1)S(1)}, u32[]{:S(2)}, u32[]{:S(2)}) collective-permute-start(bf16[3,128,704]{1,2,0:T(8,128)(2,1)S(1)} %pad_maximum_fusion.2), channel_id=1, source_target_pairs={{0,2},{1,3},{2,0},{3,1},{4,6},{5,7},{6,4},{7,5},{8,10},{9,11},{10,... | collective-permute-start | bytes 1622024 | tf_op jit(solution)/shard_map/ppermute | solution.py:517
  50.0 27.1 %copy-start.41 = (bf16[3,32,4]{1,2,0:T(4,128)(2,1)S(1)}, bf16[3,32,4]{1,2,0:T(4,128)(2,1)}, u32[]{:S(2)}) copy-start(bf16[3,32,4]{1,2,0:T(4,128)(2,1)} %param.21) | copy-start | bytes 2308
  50.0 27.4 %copy-start.43 = (s32[1,1024]{1,0:T(1,128)S(1)}, s32[1,1024]{1,0:T(1,128)}, u32[]{:S(2)}) copy-start(s32[1,1024]{1,0:T(1,128)} %param.13) | copy-start | bytes 12292
  50.0 27.4 %copy-start.44 = (s32[1,1024]{1,0:T(1,128)S(1)}, s32[1,1024]{1,0:T(1,128)}, u32[]{:S(2)}) copy-start(s32[1,1024]{1,0:T(1,128)} %param.14) | copy-start | bytes 12292
  50.0 27.4 %copy-start.45 = (s32[1,1024]{1,0:T(1,128)S(1)}, s32[1,1024]{1,0:T(1,128)}, u32[]{:S(2)}) copy-start(s32[1,1024]{1,0:T(1,128)} %param.16) | copy-start | bytes 12292
  50.0 131.8 %all-gather.9.cloned.1.call-start = ((), (), s32[]{:S(2)}) async-start(), calls=%async_computation.4 | async-start | bytes 5308416 | tf_op jit(solution)/shard_map/all_gather | solution.py:602
  51.2 326.2 %reduce-scatter.9.cloned.1.call-start = ((), (), s32[]{:S(2)}) async-start(), calls=%async_computation.7 | async-start | bytes 5308416
  52.2 24.9 %collective-permute-start.1 = (bf16[1,256,1024]{2,1,0:T(8,128)(2,1)S(1)}, bf16[1,256,1024]{2,1,0:T(8,128)(2,1)S(1)}, u32[]{:S(2)}, u32[]{:S(2)}) collective-permute-start(bf16[1,256,1024]{2,1,0:T(8,128)(2,1)S(1)} %fusion.18), channel_id=1, source_target_pairs={{0,2},{1,3},{2,0},{3,1},{4,6},{5,7},{6,4},{7,5},{8,10},{9,11},{10,... | collective-permute-start | bytes 1572872 | tf_op jit(solution)/shard_map/ppermute | solution.py:517
  52.3 25.7 %collective-permute-start = (bf16[1,256,1024]{2,1,0:T(8,128)(2,1)S(1)}, bf16[1,256,1024]{2,1,0:T(8,128)(2,1)S(1)}, u32[]{:S(2)}, u32[]{:S(2)}) collective-permute-start(bf16[1,256,1024]{2,1,0:T(8,128)(2,1)S(1)} %fusion.18), channel_id=1, source_target_pairs={{0,1},{1,0},{2,3},{3,2},{4,5},{5,4},{6,7},{7,6},{8,9},{9,8},{10,11... | collective-permute-start | bytes 1572872 | tf_op jit(solution)/shard_map/ppermute | solution.py:517
  77.1 11.6 %collective-permute-start.2 = (bf16[1,256,1024]{2,1,0:T(8,128)(2,1)S(1)}, bf16[1,256,1024]{2,1,0:T(8,128)(2,1)S(1)}, u32[]{:S(2)}, u32[]{:S(2)}) collective-permute-start(bf16[1,256,1024]{2,1,0:T(8,128)(2,1)S(1)} %collective-permute-done.1), channel_id=1, source_target_pairs={{0,1},{1,0},{2,3},{3,2},{4,5},{5,4},{6,7},{7,6},{8,9},{9,8},{10,11... | collective-permute-start | bytes 1572872 | tf_op jit(solution)/shard_map/ppermute | solution.py:517
  77.4 15.8 %copy-start.1 = (s32[1,8,1024]{2,1,0:T(8,128)}, s32[1,8,1024]{2,1,0:T(8,128)S(1)}, u32[]{:S(2)}) copy-start(s32[1,8,1024]{2,1,0:T(8,128)S(1)} %stack.67.labr) | copy-start | bytes 98308
  77.6 15.6 %copy-start = (s32[1,8,1024]{1,2,0:T(8,128)}, s32[1,8,1024]{1,2,0:T(8,128)S(1)}, u32[]{:S(2)}) copy-start(s32[1,8,1024]{1,2,0:T(8,128)S(1)} %copy.73) | copy-start | bytes 98308
  77.7 15.6 %copy-start.3 = (f32[2,4]{1,0:T(2,128)}, f32[2,4]{1,0:T(2,128)S(1)}, u32[]{:S(2)}) copy-start(f32[2,4]{1,0:T(2,128)S(1)} %maximum_convert_fusion.far) | copy-start | bytes 100
  77.7 15.5 %copy-start.2 = (f32[12,128]{1,0:T(8,128)}, f32[12,128]{1,0:T(8,128)S(1)}, u32[]{:S(2)}) copy-start(f32[12,128]{1,0:T(8,128)S(1)} %pad_convert_fusion.tab) | copy-start | bytes 18436
  93.2 34.4 %copy-start.4 = (bf16[1,1024,768]{2,1,0:T(8,128)(2,1)}, bf16[1,1024,768]{2,1,0:T(8,128)(2,1)S(1)}, u32[]{:S(2)}) copy-start(bf16[1,1024,768]{2,1,0:T(8,128)(2,1)S(1)} %fusion.9.q.k.v) | copy-start | bytes 4718596
  93.3 40.4 %copy-start.20 = (bf16[1,256,1024]{2,1,0:T(8,128)(2,1)S(1)}, bf16[1,256,1024]{2,1,0:T(8,128)(2,1)}, u32[]{:S(2)}) copy-start(bf16[1,256,1024]{2,1,0:T(8,128)(2,1)} %param.23) | copy-start | bytes 1572868
  129.3 8.2 %collective-permute-start.5 = (bf16[1,256,256]{2,1,0:T(8,128)(2,1)S(1)}, bf16[1,256,256]{2,1,0:T(8,128)(2,1)S(1)}, u32[]{:S(2)}, u32[]{:S(2)}) collective-permute-start(bf16[1,256,256]{2,1,0:T(8,128)(2,1)S(1)} %get-tuple-element.80), channel_id=1, source_target_pairs={{0,3},{1,2},{2,1},{3,0},{4,7},{5,6},{6,5},{7,4},{8,11},{9,10},{10,... | collective-permute-start | bytes 393224 | tf_op jit(solution)/shard_map/ppermute | solution.py:517
  132.8 10.6 %collective-permute-start.4 = (bf16[1,256,256]{2,1,0:T(8,128)(2,1)S(1)}, bf16[1,256,256]{2,1,0:T(8,128)(2,1)S(1)}, u32[]{:S(2)}, u32[]{:S(2)}) collective-permute-start(bf16[1,256,256]{2,1,0:T(8,128)(2,1)S(1)} %get-tuple-element.81), channel_id=1, source_target_pairs={{0,2},{1,3},{2,0},{3,1},{4,6},{5,7},{6,4},{7,5},{8,10},{9,11},{10,... | collective-permute-start | bytes 393224 | tf_op jit(solution)/shard_map/ppermute | solution.py:517
  132.8 10.6 %collective-permute-start.3 = (bf16[1,256,256]{2,1,0:T(8,128)(2,1)S(1)}, bf16[1,256,256]{2,1,0:T(8,128)(2,1)S(1)}, u32[]{:S(2)}, u32[]{:S(2)}) collective-permute-start(bf16[1,256,256]{2,1,0:T(8,128)(2,1)S(1)} %get-tuple-element.82), channel_id=1, source_target_pairs={{0,1},{1,0},{2,3},{3,2},{4,5},{5,4},{6,7},{7,6},{8,9},{9,8},{10,11... | collective-permute-start | bytes 393224 | tf_op jit(solution)/shard_map/ppermute | solution.py:517
  133.7 20.2 %collective-permute-start.10 = (bf16[1,256,1024]{2,1,0:T(8,128)(2,1)S(1)}, bf16[1,256,1024]{2,1,0:T(8,128)(2,1)S(1)}, u32[]{:S(2)}, u32[]{:S(2)}) collective-permute-start(bf16[1,256,1024]{2,1,0:T(8,128)(2,1)S(1)} %copy-done.20), channel_id=1, source_target_pairs={{0,1},{1,0},{2,3},{3,2},{4,5},{5,4},{6,7},{7,6},{8,9},{9,8},{10,11... | collective-permute-start | bytes 1572872 | tf_op jit(solution)/shard_map/ppermute | solution.py:517
  145.9 19.1 %copy-start.46 = (f32[256]{0:T(256)}, f32[256]{0:T(256)S(1)}, u32[]{:S(2)}) copy-start(f32[256]{0:T(256)S(1)} %get-tuple-element.93) | copy-start | bytes 3076
  146.0 19.1 %copy-start.39 = (f32[256]{0:T(256)}, f32[256]{0:T(256)S(1)}, u32[]{:S(2)}) copy-start(f32[256]{0:T(256)S(1)} %fusion.71) | copy-start | bytes 3076
  147.1 16.9 %collective-permute-start.9 = (bf16[1,256,1024]{2,1,0:T(8,128)(2,1)S(1)}, bf16[1,256,1024]{2,1,0:T(8,128)(2,1)S(1)}, u32[]{:S(2)}, u32[]{:S(2)}) collective-permute-start(bf16[1,256,1024]{2,1,0:T(8,128)(2,1)S(1)} %multiply_convert_fusion), channel_id=1, source_target_pairs={{0,1},{1,0},{2,3},{3,2},{4,5},{5,4},{6,7},{7,6},{8,9},{9,8},{10,11... | collective-permute-start | bytes 1572872 | tf_op jit(solution)/shard_map/ppermute | solution.py:517
  179.9 215.8 %reduce-scatter.7.cloned.1.call-start = ((), (), s32[]{:S(2)}) async-start(), calls=%async_computation.6 | async-start | bytes 5308416
  181.8 14.6 %copy-start.17 = (f32[512,1024]{1,0:T(8,128)S(1)}, f32[512,1024]{1,0:T(8,128)}, u32[]{:S(2)}) copy-start(f32[512,1024]{1,0:T(8,128)} %get-tuple-element.23) | copy-start | bytes 6291460
  199.5 15.1 %collective-permute-start.13 = (bf16[1,256,1024]{2,1,0:T(8,128)(2,1)}, bf16[1,256,1024]{2,1,0:T(8,128)(2,1)S(1)}, u32[]{:S(2)}, u32[]{:S(2)}) collective-permute-start(bf16[1,256,1024]{2,1,0:T(8,128)(2,1)} %slice.139), channel_id=1, source_target_pairs={{0,1},{1,0},{2,3},{3,2},{4,5},{5,4},{6,7},{7,6},{8,9},{9,8},{10,11... | collective-permute-start | bytes 1572872 | tf_op jit(solution)/shard_map/ppermute | solution.py:517
  203.8 20.0 %collective-permute-start.12 = (bf16[1,256,1024]{2,1,0:T(8,128)(2,1)}, bf16[1,256,1024]{2,1,0:T(8,128)(2,1)}, u32[]{:S(2)}, u32[]{:S(2)}) collective-permute-start(bf16[1,256,1024]{2,1,0:T(8,128)(2,1)} %slice.140), channel_id=1, source_target_pairs={{0,1},{1,0},{2,3},{3,2},{4,5},{5,4},{6,7},{7,6},{8,9},{9,8},{10,11... | collective-permute-start | bytes 1572872 | tf_op jit(solution)/shard_map/ppermute | solution.py:517
  209.6 14.2 %copy-start.11 = (f32[1,256,1024]{2,1,0:T(8,128)S(1)}, f32[1,256,1024]{2,1,0:T(8,128)}, u32[]{:S(2)}) copy-start(f32[1,256,1024]{2,1,0:T(8,128)} %copy-done.10) | copy-start | bytes 3145732
  209.7 14.2 %copy-start.21 = (bf16[1,256,1024]{2,1,0:T(8,128)(2,1)S(1)}, bf16[1,256,1024]{2,1,0:T(8,128)(2,1)}, u32[]{:S(2)}) copy-start(bf16[1,256,1024]{2,1,0:T(8,128)(2,1)} %param.23) | copy-start | bytes 1572868
  209.7 14.1 %copy-start.40 = (f32[256]{0:T(256)S(1)}, f32[256]{0:T(256)}, u32[]{:S(2)}) copy-start(f32[256]{0:T(256)} %copy-done.39) | copy-start | bytes 3076
  231.1 8.4 %collective-permute-start.16 = (bf16[1,256,256]{2,1,0:T(8,128)(2,1)S(1)}, bf16[1,256,256]{2,1,0:T(8,128)(2,1)S(1)}, u32[]{:S(2)}, u32[]{:S(2)}) collective-permute-start(bf16[1,256,256]{2,1,0:T(8,128)(2,1)S(1)} %get-tuple-element.76), channel_id=1, source_target_pairs={{0,3},{1,2},{2,1},{3,0},{4,7},{5,6},{6,5},{7,4},{8,11},{9,10},{10,... | collective-permute-start | bytes 393224 | tf_op jit(solution)/shard_map/ppermute | solution.py:517
  235.3 9.5 %collective-permute-start.15 = (bf16[1,256,256]{2,1,0:T(8,128)(2,1)S(1)}, bf16[1,256,256]{2,1,0:T(8,128)(2,1)S(1)}, u32[]{:S(2)}, u32[]{:S(2)}) collective-permute-start(bf16[1,256,256]{2,1,0:T(8,128)(2,1)S(1)} %get-tuple-element.77), channel_id=1, source_target_pairs={{0,2},{1,3},{2,0},{3,1},{4,6},{5,7},{6,4},{7,5},{8,10},{9,11},{10,... | collective-permute-start | bytes 393224 | tf_op jit(solution)/shard_map/ppermute | solution.py:517
  235.3 9.5 %collective-permute-start.14 = (bf16[1,256,256]{2,1,0:T(8,128)(2,1)S(1)}, bf16[1,256,256]{2,1,0:T(8,128)(2,1)S(1)}, u32[]{:S(2)}, u32[]{:S(2)}) collective-permute-start(bf16[1,256,256]{2,1,0:T(8,128)(2,1)S(1)} %get-tuple-element.78), channel_id=1, source_target_pairs={{0,1},{1,0},{2,3},{3,2},{4,5},{5,4},{6,7},{7,6},{8,9},{9,8},{10,11... | collective-permute-start | bytes 393224 | tf_op jit(solution)/shard_map/ppermute | solution.py:517
  237.9 110.4 %collective-permute-start.23 = (bf16[4,128,1024]{2,1,0:T(8,128)(2,1)}, bf16[4,128,1024]{2,1,0:T(8,128)(2,1)}, u32[]{:S(2)}, u32[]{:S(2)}) collective-permute-start(bf16[4,128,1024]{2,1,0:T(8,128)(2,1)} %fusion.20), channel_id=1, source_target_pairs={{0,4},{4,0},{8,12},{12,8},{16,20},{20,16},{24,28},{28,24},{1,5},{5... | collective-permute-start | bytes 3145736 | tf_op jit(solution)/shard_map/ppermute | solution.py:517
  245.8 60.8 %copy-start.19 = (bf16[1024,1024]{1,0:T(8,128)(2,1)S(1)}, bf16[1024,1024]{1,0:T(8,128)(2,1)}, u32[]{:S(2)}) copy-start(bf16[1024,1024]{1,0:T(8,128)(2,1)} %copy.81) | copy-start | bytes 6291460
  306.5 15.2 %collective-permute-start.30 = (bf16[4,12,4]{1,2,0:T(4,128)(2,1)S(1)}, bf16[4,12,4]{1,2,0:T(4,128)(2,1)S(1)}, u32[]{:S(2)}, u32[]{:S(2)}) collective-permute-start(bf16[4,12,4]{1,2,0:T(4,128)(2,1)S(1)} %fusion.41), channel_id=1, source_target_pairs={{0,4},{4,0},{8,12},{12,8},{16,20},{20,16},{24,28},{28,24},{1,5},{5... | collective-permute-start | bytes 1160 | tf_op jit(solution)/shard_map/ppermute | solution.py:517
  316.7 25.2 %collective-permute-start.20 = (bf16[4,128,768]{2,1,0:T(8,128)(2,1)}, bf16[4,128,768]{2,1,0:T(8,128)(2,1)}, u32[]{:S(2)}, u32[]{:S(2)}) collective-permute-start(bf16[4,128,768]{2,1,0:T(8,128)(2,1)} %fusion.27), channel_id=1, source_target_pairs={{0,4},{4,0},{8,12},{12,8},{16,20},{20,16},{24,28},{28,24},{1,5},{5... | collective-permute-start | bytes 2359304 | tf_op jit(solution)/shard_map/ppermute | solution.py:517
  321.8 3.7 collective-permute-start.31
  323.4 15.0 %collective-permute-start.18 = (bf16[1,256,1024]{2,1,0:T(8,128)(2,1)}, bf16[1,256,1024]{2,1,0:T(8,128)(2,1)S(1)}, u32[]{:S(2)}, u32[]{:S(2)}) collective-permute-start(bf16[1,256,1024]{2,1,0:T(8,128)(2,1)} %bitcast.221), channel_id=1, source_target_pairs={{0,1},{1,0},{2,3},{3,2},{4,5},{5,4},{6,7},{7,6},{8,9},{9,8},{10,11... | collective-permute-start | bytes 1572872 | tf_op jit(solution)/shard_map/ppermute | solution.py:517
  323.4 33.2 %collective-permute-start.17 = (bf16[1,256,1024]{2,1,0:T(8,128)(2,1)}, bf16[1,256,1024]{2,1,0:T(8,128)(2,1)}, u32[]{:S(2)}, u32[]{:S(2)}) collective-permute-start(bf16[1,256,1024]{2,1,0:T(8,128)(2,1)} %bitcast.220), channel_id=1, source_target_pairs={{0,1},{1,0},{2,3},{3,2},{4,5},{5,4},{6,7},{7,6},{8,9},{9,8},{10,11... | collective-permute-start | bytes 1572872 | tf_op jit(solution)/shard_map/ppermute | solution.py:517
  325.4 3.6 collective-permute-start.32
  340.6 24.0 %collective-permute-start.19 = (bf16[1,256,1024]{2,1,0:T(8,128)(2,1)}, bf16[1,256,1024]{2,1,0:T(8,128)(2,1)}, u32[]{:S(2)}, u32[]{:S(2)}) collective-permute-start(bf16[1,256,1024]{2,1,0:T(8,128)(2,1)} %fusion.24), channel_id=1, source_target_pairs={{0,2},{1,3},{2,0},{3,1},{4,6},{5,7},{6,4},{7,5},{8,10},{9,11},{10,... | collective-permute-start | bytes 1572872 | tf_op jit(solution)/shard_map/ppermute | solution.py:517
  347.9 18.3 %collective-permute-start.21 = (bf16[2,128,768]{1,2,0:T(8,128)(2,1)}, bf16[2,128,768]{1,2,0:T(8,128)(2,1)}, u32[]{:S(2)}, u32[]{:S(2)}) collective-permute-start(bf16[2,128,768]{1,2,0:T(8,128)(2,1)} %bitcast.191), channel_id=1, source_target_pairs={{0,8},{4,12},{8,0},{12,4},{16,24},{20,28},{24,16},{28,20},{1,9},{5... | collective-permute-start | bytes 1179656 | tf_op jit(solution)/shard_map/ppermute | solution.py:517
  354.6 11.5 %copy-start.15 = (f32[2,1,128,768]{2,3,0,1:T(8,128)S(1)}, f32[2,1,128,768]{2,3,0,1:T(8,128)}, u32[]{:S(2)}) copy-start(f32[2,1,128,768]{2,3,0,1:T(8,128)} %copy.82) | copy-start | bytes 2359300
  354.9 13.6 %copy-start.14 = (f32[2,1,128,1024]{2,3,0,1:T(8,128)S(1)}, f32[2,1,128,1024]{2,3,0,1:T(8,128)}, u32[]{:S(2)}) copy-start(f32[2,1,128,1024]{2,3,0,1:T(8,128)} %copy.85) | copy-start | bytes 3145732
  354.9 13.6 %collective-permute-start.24 = (bf16[2,128,1024]{1,2,0:T(8,128)(2,1)S(1)}, bf16[2,128,1024]{1,2,0:T(8,128)(2,1)S(1)}, u32[]{:S(2)}, u32[]{:S(2)}) collective-permute-start(bf16[2,128,1024]{1,2,0:T(8,128)(2,1)S(1)} %bitcast.222), channel_id=1, source_target_pairs={{0,8},{4,12},{8,0},{12,4},{16,24},{20,28},{24,16},{28,20},{1,9},{5... | collective-permute-start | bytes 1572872 | tf_op jit(solution)/shard_map/ppermute | solution.py:517
  367.3 7.2 %collective-permute-start.22 = (bf16[1,128,768]{1,2,0:T(8,128)(2,1)S(1)}, bf16[1,128,768]{1,2,0:T(8,128)(2,1)S(1)}, u32[]{:S(2)}, u32[]{:S(2)}) collective-permute-start(bf16[1,128,768]{1,2,0:T(8,128)(2,1)S(1)} %dynamic-slice_convert_fusion.3), channel_id=1, source_target_pairs={{0,16},{4,20},{8,24},{12,28},{16,0},{20,4},{24,8},{28,12},{1,17},{... | collective-permute-start | bytes 589832 | tf_op jit(solution)/shard_map/ppermute | solution.py:517
  368.6 8.6 %collective-permute-start.25 = (bf16[1,128,1024]{1,2,0:T(8,128)(2,1)S(1)}, bf16[1,128,1024]{1,2,0:T(8,128)(2,1)S(1)}, u32[]{:S(2)}, u32[]{:S(2)}) collective-permute-start(bf16[1,128,1024]{1,2,0:T(8,128)(2,1)S(1)} %dynamic-slice_convert_fusion.2), channel_id=1, source_target_pairs={{0,16},{4,20},{8,24},{12,28},{16,0},{20,4},{24,8},{28,12},{1,17},{... | collective-permute-start | bytes 786440 | tf_op jit(solution)/shard_map/ppermute | solution.py:517
  377.3 19.7 %copy-start.33 = (f32[128,1024]{0,1:T(8,128)}, f32[128,1024]{0,1:T(8,128)S(1)}, u32[]{:S(2)}) copy-start(f32[128,1024]{0,1:T(8,128)S(1)} %get-tuple-element.57) | copy-start | bytes 1572868
  378.9 25.4 %collective-permute-start.29 = (bf16[384,704]{0,1:T(8,128)(2,1)S(1)}, bf16[384,704]{0,1:T(8,128)(2,1)S(1)}, u32[]{:S(2)}, u32[]{:S(2)}) collective-permute-start(bf16[384,704]{0,1:T(8,128)(2,1)S(1)} %copy.105), channel_id=1, source_target_pairs={{0,2},{1,3},{2,0},{3,1},{4,6},{5,7},{6,4},{7,5},{8,10},{9,11},{10,... | collective-permute-start | bytes 1622024 | tf_op jit(solution)/shard_map/ppermute | solution.py:517
  379.6 11.5 %collective-permute-start.27 = (bf16[128,256]{0,1:T(8,128)(2,1)S(1)}, bf16[128,256]{0,1:T(8,128)(2,1)S(1)}, u32[]{:S(2)}, u32[]{:S(2)}) collective-permute-start(bf16[128,256]{0,1:T(8,128)(2,1)S(1)} %get-tuple-element.84), channel_id=1, source_target_pairs={{0,1},{1,0},{2,3},{3,2},{4,5},{5,4},{6,7},{7,6},{8,9},{9,8},{10,11... | collective-permute-start | bytes 196616 | tf_op jit(solution)/shard_map/ppermute | solution.py:517
  382.6 25.9 %collective-permute-start.26 = (bf16[128,256]{0,1:T(8,128)(2,1)S(1)}, bf16[128,256]{0,1:T(8,128)(2,1)S(1)}, u32[]{:S(2)}, u32[]{:S(2)}) collective-permute-start(bf16[128,256]{0,1:T(8,128)(2,1)S(1)} %get-tuple-element.83), channel_id=1, source_target_pairs={{0,1},{1,0},{2,3},{3,2},{4,5},{5,4},{6,7},{7,6},{8,9},{9,8},{10,11... | collective-permute-start | bytes 196616 | tf_op jit(solution)/shard_map/ppermute | solution.py:517
  391.1 17.4 %collective-permute-start.28 = (bf16[128,256]{0,1:T(8,128)(2,1)S(1)}, bf16[128,256]{0,1:T(8,128)(2,1)S(1)}, u32[]{:S(2)}, u32[]{:S(2)}) collective-permute-start(bf16[128,256]{0,1:T(8,128)(2,1)S(1)} %fusion.35), channel_id=1, source_target_pairs={{0,2},{1,3},{2,0},{3,1},{4,6},{5,7},{6,4},{7,5},{8,10},{9,11},{10,... | collective-permute-start | bytes 196616 | tf_op jit(solution)/shard_map/ppermute | solution.py:517
  408.4 3.7 collective-permute-start.34
  410.1 4.2 collective-permute-start.33
  412.1 4.5 %collective-permute-start.35 = (f32[2,32]{1,0:T(2,128)S(1)}, f32[2,32]{1,0:T(2,128)S(1)}, u32[]{:S(2)}, u32[]{:S(2)}) collective-permute-start(f32[2,32]{1,0:T(2,128)S(1)} %add.400), channel_id=1, source_target_pairs={{0,2},{1,3},{2,0},{3,1},{4,6},{5,7},{6,4},{7,5},{8,10},{9,11},{10,... | collective-permute-start | bytes 776 | tf_op jit(solution)/shard_map/ppermute | solution.py:517
  (28 other events, 113.0 us)
Sparse Core Ops, SparseCore 0:
  9.9 28.5 all-gather.4
  40.9 28.1 all-gather.6
  71.1 38.9 all-gather.10
  112.3 38.9 all-gather.8
  180.0 54.6 reduce-scatter.8
  238.4 53.9 reduce-scatter.6
